TPU v7x, 32 devices: a whole 2x2x4 slice. The times are simulated.
32 devices in a mesh: tm: 4 (over x, core), mem: 8 (over z, y).
Axes of the slice: x: 2, y: 2, z: 4, core: 2. Of those that a mesh axis runs over, the one named last changes fastest.
Arguments:
- tokens: bfloat16 [8192, 2048], P(('tm', 'mem')), may hold values from -6 to 6
- queries: bfloat16 [8192, 2048], P(('tm', 'mem')), may hold values from -6 to 6
- log_decay: bfloat16 [8192, 16], P(('tm', 'mem')), may hold values from -1 to 0
- route_ids: int32 [8192, 2], P(('tm', 'mem')), may hold values from 0 to 7, all different within a row; in each aligned block of 256 rows (0 to 255, 256 to 511, ...) at most 96 rows name the same one
- gate_weights: float32 [8192, 2], P(('tm', 'mem')), may hold values from 0.3 to 1
- kv_weight: bfloat16 [8, 2048, 4096], P('mem'), may hold values from -0.125 to 0.125
Outputs:
- mixed: bfloat16 [8192, 2048], P(('tm', 'mem'))
Inputs may be any that keep to these rules, and one draw needn't show every extreme that they name: `route_ids`: each row names 2 different memories. In each aligned block of 256 rows (the rows of one device) no memory is named by more than 96 rows, and in some block one memory is named by exactly 96 rows.
All inputs are finite; a program needn't handle non-finite values.
Results may differ from a plain program's by a relative error of at most 0.006.
Values may be sent and summed in bfloat16 or wider, within the bound.
No kernel may reach another device: no remote copies, remote signals or barrier semaphores. Data moves between devices by JAX's collectives and lax.ppermute only.
A program may use at most 128 MiB of HBM per device.

v0:
```python
import math

import jax
import jax.numpy as jnp
from jax import lax
from jax.sharding import PartitionSpec as P

exact_mode = lax.Precision.HIGHEST


def prefix(part, axis, combine, identity):
    place = lax.axis_index(axis)
    gathered = jax.tree.map(lambda a: lax.all_gather(a, axis), part)
    state = jax.tree.map(lambda a, e: jnp.zeros_like(a) + jnp.asarray(e, a.dtype), part, identity)

    def one(turn, state):
        return combine(
            state, jax.tree.map(lambda a: lax.dynamic_index_in_dim(a, turn, 0, False), gathered)
        )

    return lax.fori_loop(0, place, one, state)


def block_pass(queries_heads, keys_heads, values_heads, decay_logs, block_rows):
    head_count, chain_rows, head_size = queries_heads.shape
    block_count = chain_rows // block_rows

    def split_blocks(tensor):
        return jnp.moveaxis(tensor.reshape(head_count, block_count, block_rows, head_size), 1, 0)

    blocked = (
        split_blocks(queries_heads),
        split_blocks(keys_heads),
        split_blocks(values_heads),
        jnp.moveaxis(decay_logs.reshape(head_count, block_count, block_rows), 1, 0),
    )
    lower = jnp.arange(block_rows)[:, None] >= jnp.arange(block_rows)[None, :]

    def advance(carried, pieces):
        query_block, key_block, value_block, log_block = pieces
        running = jnp.cumsum(log_block, axis=1)
        spread = jnp.minimum(running[:, :, None] - running[:, None, :], 0.0)
        weights = jnp.where(lower[None], jnp.exp(spread), 0.0)
        scores = (
            jnp.einsum("hnd,hid->hni", query_block, key_block, preferred_element_type=jnp.float32)
            * weights
        )
        value_wide = value_block.astype(jnp.float32)
        within = jnp.einsum("hni,hie->hne", scores, value_wide, precision=exact_mode)
        earlier = (
            jnp.einsum(
                "hnd,hde->hne", query_block.astype(jnp.float32), carried, precision=exact_mode
            )
            * jnp.exp(running)[:, :, None]
        )
        ending = running[:, -1]
        fading = jnp.exp(ending[:, None] - running)
        carried = jnp.exp(ending)[:, None, None] * carried + jnp.einsum(
            "hid,hie->hde",
            key_block.astype(jnp.float32) * fading[:, :, None],
            value_wide,
            precision=exact_mode,
        )
        return (carried, within + earlier)

    start = jnp.zeros((head_count, head_size, head_size), jnp.float32)
    final_state, outputs = lax.scan(advance, start, blocked)
    outputs = jnp.moveaxis(outputs, 0, 1).reshape(head_count, chain_rows, head_size)
    return (final_state, outputs)


def normalize(outputs):
    mean_square = jnp.mean(outputs * outputs, axis=-1, keepdims=True)
    return outputs * lax.rsqrt(mean_square + 1e-06)


def link(earlier_pair, later_pair):
    return (
        earlier_pair[0] + later_pair[0],
        jnp.exp(later_pair[0])[:, None, None] * earlier_pair[1] + later_pair[1],
    )


def on_device(tokens, queries, log_decay, route_ids, gate_weights, kv_weight):
    tok_rows, model_width = tokens.shape
    head_count = log_decay.shape[1]
    head_size = model_width // head_count
    top_count = route_ids.shape[1]
    members = lax.axis_size("mem")
    capacity = 3 * tok_rows * top_count // (2 * members)
    chain_rows = members * capacity
    flat_ids = route_ids.reshape(-1)
    onehot = (flat_ids[:, None] == jnp.arange(members, dtype=jnp.int32)[None, :]).astype(jnp.int32)
    before = jnp.cumsum(onehot, axis=0) - onehot
    position = jnp.sum(before * onehot, axis=1)
    slot_index = flat_ids * capacity + position
    source_row = jnp.arange(flat_ids.shape[0], dtype=jnp.int32) // top_count
    slot_token = jnp.full((chain_rows,), tok_rows, jnp.int32).at[slot_index].set(source_row)
    padded_tokens = jnp.concatenate([tokens, jnp.zeros((1, model_width), jnp.bfloat16)], axis=0)
    padded_queries = jnp.concatenate([queries, jnp.zeros((1, model_width), jnp.bfloat16)], axis=0)
    padded_decay = jnp.concatenate([log_decay, jnp.zeros((1, head_count), jnp.bfloat16)], axis=0)
    send_tokens = padded_tokens[slot_token].reshape(members, capacity, model_width)
    send_queries = padded_queries[slot_token].reshape(members, capacity, model_width)
    send_decay = padded_decay[slot_token].reshape(members, capacity, head_count)
    received_tokens, received_queries, received_decay = (
        lax.all_to_all(send_tokens, "mem", split_axis=0, concat_axis=0, tiled=True),
        lax.all_to_all(send_queries, "mem", split_axis=0, concat_axis=0, tiled=True),
        lax.all_to_all(send_decay, "mem", split_axis=0, concat_axis=0, tiled=True),
    )
    chain_x = received_tokens.reshape(chain_rows, model_width)
    projected = jnp.dot(chain_x, kv_weight[0], preferred_element_type=jnp.float32).astype(
        jnp.bfloat16
    )
    keys_heads = (
        projected[:, :model_width].reshape(chain_rows, head_count, head_size).transpose(1, 0, 2)
    )
    values_heads = (
        projected[:, model_width:].reshape(chain_rows, head_count, head_size).transpose(1, 0, 2)
    )
    keys_heads, values_heads = (keys_heads, values_heads)
    query_heads = received_queries.reshape(chain_rows, head_count, head_size).transpose(1, 0, 2)
    logs_heads = received_decay.reshape(chain_rows, head_count).astype(jnp.float32).T
    block_rows = math.gcd(chain_rows, 512)
    final_local, local_out = block_pass(
        query_heads, keys_heads, values_heads, logs_heads, block_rows
    )
    total_log = jnp.sum(logs_heads, axis=1)
    identity = (
        jnp.zeros((head_count,), jnp.float32),
        jnp.zeros((head_count, head_size, head_size), jnp.float32),
    )
    incoming_log, incoming = prefix((total_log, final_local), "tm", link, identity)
    through = jnp.cumsum(logs_heads, axis=1)
    outputs = local_out + jnp.exp(through)[:, :, None] * jnp.einsum(
        "hnd,hde->hne", query_heads.astype(jnp.float32), incoming, precision=exact_mode
    )
    normed = (
        normalize(outputs)
        .astype(jnp.bfloat16)
        .transpose(1, 0, 2)
        .reshape(members, capacity, model_width)
    )
    returned = lax.all_to_all(normed, "mem", split_axis=0, concat_axis=0, tiled=True)
    picked = returned.reshape(chain_rows, model_width)[slot_index].astype(jnp.float32)
    picked = picked.reshape(tok_rows, top_count, model_width)
    mixed = jnp.sum(gate_weights[:, :, None] * picked, axis=1)
    return mixed.astype(jnp.bfloat16)


def solution(mesh):
    placed = (
        P(("tm", "mem"), None),
        P(("tm", "mem"), None),
        P(("tm", "mem"), None),
        P(("tm", "mem"), None),
        P(("tm", "mem"), None),
        P("mem", None, None),
    )
    return jax.shard_map(
        on_device, mesh=mesh, in_specs=placed, out_specs=P(("tm", "mem"), None), check_vma=False
    )
```

profile of v0, /device:TPU:0, one launch (start us, length us, event | category | flops | bytes accessed | tf_op | source)
XLA Modules:
  0.0 390.3 jit_solution(5555272272936313366)
XLA Ops:
  6.5 0.9 copy.88
  7.7 0.7 broadcast_multiply_fusion
  8.4 1.1 reduce-window.22
  9.6 0.2 slice_reduce_fusion.3
  10.2 2.4 scatter_custom_fusion
  12.7 0.8 copy.86
  13.5 1.9 gather_fusion
  15.4 0.7 copy.90
  16.2 7.3 %all-to-all-start = ((bf16[8,96,16]{1,2,0:T(8,128)(2,1)}), bf16[8,96,16]{1,2,0:T(8,128)(2,1)S(1)}, u32[]{:S(2)}, u32[]{:S(2)}) async-start(bf16[8,96,16]{1,2,0:T(8,128)(2,1)} %copy.90), calls=%async_computation | async-start | bytes 65536 | tf_op jit(solution)/shard_map/all_to_all | solution.py:108
  23.6 4.4 %gather_fusion.1 = bf16[768,2048]{1,0:T(8,128)(2,1)} fusion(bf16[257,2048]{1,0:T(8,128)(2,1)S(1)} %concatenate.10, s32[1024]{0:T(1024)S(1)} %pad_clamp_fusion.1), kind=kCustom, calls=%fused_computation.1 | custom fusion | bytes 6294528 | tf_op jit(solution)/shard_map/gather | solution.py:102
  28.0 2.2 all-to-all-done
  30.2 4.6 %all-to-all-start.1 = ((bf16[8,96,2048]{2,1,0:T(8,128)(2,1)}), bf16[8,96,2048]{2,1,0:T(8,128)(2,1)}, u32[]{:S(2)}, u32[]{:S(2)}) async-start(bf16[8,96,2048]{2,1,0:T(8,128)(2,1)} %bitcast.146), calls=%async_computation.1 | async-start | bytes 6291456 | tf_op jit(solution)/shard_map/all_to_all | solution.py:106
  34.9 4.3 %gather_fusion.2 = bf16[768,2048]{1,0:T(8,128)(2,1)} fusion(bf16[257,2048]{1,0:T(8,128)(2,1)S(1)} %concatenate.11, s32[1024]{0:T(1024)S(1)} %pad_clamp_fusion.1), kind=kCustom, calls=%fused_computation.2 | custom fusion | bytes 6294528 | tf_op jit(solution)/shard_map/gather | solution.py:103
  39.2 65.2 %all-to-all-done.1 = bf16[8,96,2048]{2,1,0:T(8,128)(2,1)} async-done(((bf16[8,96,2048]{2,1,0:T(8,128)(2,1)}), bf16[8,96,2048]{2,1,0:T(8,128)(2,1)}, u32[]{:S(2)}, u32[]{:S(2)}) %all-to-all-start.1) | async-done | bytes 3145760 | tf_op jit(solution)/shard_map/all_to_all | solution.py:106
  104.3 3.6 all-to-all-start.2
  108.0 0.6 all-gather.4.cloned.1.call-start
  108.7 17.6 %fusion.34 = bf16[768,4096]{1,0:T(8,128)(2,1)S(1)} fusion(bf16[768,2048]{1,0:T(8,128)(2,1)} %bitcast.10, bf16[1,2048,4096]{2,1,0:T(8,128)(2,1)} %param.15), kind=kOutput, calls=%fused_computation.50 | convolution fusion | flops 12888047616 | bytes 26214400 | tf_op jit(solution)/shard_map/dot_general | solution.py:111
  126.4 2.6 slice_bitcast_fusion
  129.0 2.7 copy.123
  131.7 2.7 copy.124
  134.4 44.5 %all-to-all-done.2 = bf16[8,96,2048]{2,1,0:T(8,128)(2,1)S(1)} async-done(((bf16[8,96,2048]{2,1,0:T(8,128)(2,1)}), bf16[8,96,2048]{2,1,0:T(8,128)(2,1)S(1)}, u32[]{:S(2)}, u32[]{:S(2)}) %all-to-all-start.2) | async-done | bytes 3145760 | tf_op jit(solution)/shard_map/all_to_all | solution.py:107
  178.9 1.0 copy.125
  179.9 2.7 copy.150
  182.5 52.2 %while.26 = (s32[]{:T(128)}, f32[16,128,128]{2,1,0:T(8,128)}, f32[3,16,256,128]{3,2,0,1:T(8,128)}, f32[3,16,256]{2,0,1:T(4,128)S(1)}, bf16[3,16,256,128]{3,1,2,0...) while((s32[]{:T(128)}, f32[16,128,128]{2,1,0:T(8,128)}, ...), condition=%wide.region_7.8_spmd.clone, body=%wide.region_4.7_spmd.clone.sunk | while | flops 3497598976 | bytes 37063800 | solution.py:67
  182.7 0.6 reduce-window.38
  183.3 0.2 slice_reduce_fusion.6
  183.6 1.9 constant_dynamic-slice_fusion.6
  185.5 2.3 fusion.70
  187.9 3.0 fusion.71
  191.0 0.2 slice_reduce_fusion.7
  191.2 3.8 bitcast_dynamic-update-slice_fusion.2
  195.1 4.1 %fusion.69 = f32[16,128,128]{2,1,0:T(8,128)} fusion(f32[16,256]{1,0:T(8,128)S(1)} %get-tuple-element.260, f32[16,128,128]{2,1,0:T(8,128)} %get-tuple-element.275, bf16[1,16,256,128]{3,1,2,0:T(8,128)(2,1)S(1)} %get-tuple-element.261, bf16[1,16,256,128]{3,1,2,0:T(8,128)(2,1)S(1)} %copy-done.2, f32[16]{0:T(128)S(1)} %exp.67, pred[]{:T(512)S(6)} %compare.8), kind=kOutput, calls=%fused_computation.22.clone.1 | convolution fusion | flops 807141376 | bytes 4210753 | tf_op jit(solution)/shard_map/while/body/eval_jaxpr/hid,hie->hde/dot_general | solution.py:58
  199.2 0.6 reduce-window.38
  199.8 0.2 slice_reduce_fusion.6
  200.1 1.9 constant_dynamic-slice_fusion.6
  202.0 2.3 fusion.70
  204.4 3.0 fusion.71
  207.4 0.2 slice_reduce_fusion.7
  207.7 4.2 %bitcast_dynamic-update-slice_fusion.2 = f32[3,16,256,128]{3,2,0,1:T(8,128)} fusion(f32[3,16,256,128]{3,2,0,1:T(8,128)} %get-tuple-element.276, s32[]{:T(128)} %get-tuple-element.274, f32[16,256,128]{2,1,0:T(8,128)S(1)} %fusion.71, f32[16,256]{1,0:T(8,128)S(1)} %get-tuple-element.263, f32[16,128,128]{2,1,0:T(8,128)} %get-tuple-element.275, ...), kind=kOutput, calls=%fused_computation.14.clone.1 | convolution fusion | flops 806617088 | bytes 6308865 | tf_op jit(solution)/shard_map/while/body/eval_jaxpr/hnd,hde->hne/dot_general | solution.py:51
  211.9 5.1 %fusion.69 = f32[16,128,128]{2,1,0:T(8,128)} fusion(f32[16,256]{1,0:T(8,128)S(1)} %get-tuple-element.260, f32[16,128,128]{2,1,0:T(8,128)} %get-tuple-element.275, bf16[1,16,256,128]{3,1,2,0:T(8,128)(2,1)S(1)} %get-tuple-element.261, bf16[1,16,256,128]{3,1,2,0:T(8,128)(2,1)S(1)} %copy-done.2, f32[16]{0:T(128)S(1)} %exp.67, pred[]{:T(512)S(6)} %compare.8), kind=kOutput, calls=%fused_computation.22.clone.1 | convolution fusion | flops 807141376 | bytes 4210753 | tf_op jit(solution)/shard_map/while/body/eval_jaxpr/hid,hie->hde/dot_general | solution.py:58
  217.0 0.6 reduce-window.38
  217.6 0.2 slice_reduce_fusion.6
  217.9 1.9 constant_dynamic-slice_fusion.6
  219.8 2.3 fusion.70
  222.2 3.0 fusion.71
  225.2 0.2 slice_reduce_fusion.7
  225.5 4.1 %bitcast_dynamic-update-slice_fusion.2 = f32[3,16,256,128]{3,2,0,1:T(8,128)} fusion(f32[3,16,256,128]{3,2,0,1:T(8,128)} %get-tuple-element.276, s32[]{:T(128)} %get-tuple-element.274, f32[16,256,128]{2,1,0:T(8,128)S(1)} %fusion.71, f32[16,256]{1,0:T(8,128)S(1)} %get-tuple-element.263, f32[16,128,128]{2,1,0:T(8,128)} %get-tuple-element.275, ...), kind=kOutput, calls=%fused_computation.14.clone.1 | convolution fusion | flops 806617088 | bytes 6308865 | tf_op jit(solution)/shard_map/while/body/eval_jaxpr/hnd,hde->hne/dot_general | solution.py:51
  229.7 5.1 %fusion.69 = f32[16,128,128]{2,1,0:T(8,128)} fusion(f32[16,256]{1,0:T(8,128)S(1)} %get-tuple-element.260, f32[16,128,128]{2,1,0:T(8,128)} %get-tuple-element.275, bf16[1,16,256,128]{3,1,2,0:T(8,128)(2,1)S(1)} %get-tuple-element.261, bf16[1,16,256,128]{3,1,2,0:T(8,128)(2,1)S(1)} %copy-done.2, f32[16]{0:T(128)S(1)} %exp.67, pred[]{:T(512)S(6)} %compare.8), kind=kOutput, calls=%fused_computation.22.clone.1 | convolution fusion | flops 807141376 | bytes 4210753 | tf_op jit(solution)/shard_map/while/body/eval_jaxpr/hid,hie->hde/dot_general | solution.py:58
  234.8 0.7 dynamic-slice
  236.3 0.2 dynamic-update-slice
  236.5 5.6 %all-reduce.3 = f32[64]{0:T(128)S(1)} all-reduce(f32[64]{0:T(128)S(1)} %dynamic-update-slice), channel_id=2, replica_groups=mesh['tm'=4,'mem'=8] {'tm'}, use_global_device_ids=true, to_apply=%add.3 | all-reduce | flops 64 | bytes 512
  242.3 1.7 reduce-window.26
  244.3 6.6 %copy.103 = f32[16,768,128]{1,2,0:T(8,128)} copy(f32[16,768,128]{2,1,0:T(8,128)} %bitcast.148) | data formatting | bytes 12582912 | tf_op jit(solution)/shard_map/reshape | solution.py:68
  250.9 17.6 %all-gather.4.cloned.1.call-done = f32[64,128,128]{2,1,0:T(8,128)} async-done(((f32[16,128,128]{2,1,0:T(8,128)}), f32[64,128,128]{2,1,0:T(8,128)}) %all-gather.4.cloned.1.call-update) | async-done | bytes 4194320 | tf_op jit(solution)/shard_map/all_gather | solution.py:13
  268.6 0.2 while.25
  268.8 8.0 %multiply_reduce_fusion = (f32[16,768]{1,0:T(8,128)S(1)}, f32[16,768,128]{1,2,0:T(8,128)S(1)}) fusion(f32[16,768,128]{1,2,0:T(8,128)} %copy.103, f32[16,128,128]{2,1,0:T(8,128)S(1)} %get-tuple-element.94, bf16[768,16,128]{2,1,0:T(8,128)(2,1)} %bitcast.141, f32[16,768]{1,0:T(8,128)S(1)} %copy_bitcast_fusion.8), kind=kOutput, calls=%fused_computation.52 | convolution fusion | flops 2422198272 | bytes 16875520 | tf_op jit(solution)/shard_map/hnd,hde->hne/dot_general | solution.py:134
  276.8 2.4 fusion.37
  279.2 4.1 %copy.104 = bf16[768,16,128]{2,1,0:T(8,128)(2,1)S(1)} copy(bf16[768,16,128]{0,2,1:T(8,128)(2,1)} %fusion.37) | data formatting | bytes 6291456 | tf_op jit(solution)/shard_map/transpose | solution.py:140
  283.3 3.4 reshape.218
  286.7 5.9 %all-to-all-start.3 = ((bf16[8,96,2048]{2,1,0:T(8,128)(2,1)}), bf16[8,96,2048]{2,1,0:T(8,128)(2,1)S(1)}, u32[]{:S(2)}, u32[]{:S(2)}) async-start(bf16[8,96,2048]{2,1,0:T(8,128)(2,1)} %reshape.218), calls=%async_computation.3 | async-start | bytes 6291456 | tf_op jit(solution)/shard_map/all_to_all | solution.py:143
  292.8 71.8 %all-to-all-done.3 = bf16[8,96,2048]{2,1,0:T(8,128)(2,1)S(1)} async-done(((bf16[8,96,2048]{2,1,0:T(8,128)(2,1)}), bf16[8,96,2048]{2,1,0:T(8,128)(2,1)S(1)}, u32[]{:S(2)}, u32[]{:S(2)}) %all-to-all-start.3) | async-done | bytes 3145760 | tf_op jit(solution)/shard_map/all_to_all | solution.py:143
  364.6 3.3 gather_fusion.3
  367.9 5.4 %reshape.220 = f32[256,2,2048]{2,1,0:T(2,128)} reshape(bf16[512,2048]{1,0:T(8,128)(2,1)} %gather_fusion.3) | data formatting | bytes 6291456 | tf_op jit(solution)/shard_map/convert_element_type | solution.py:144
  373.3 9.9 %multiply_reduce_fusion.1 = bf16[256,2048]{1,0:T(8,128)(2,1)} fusion(f32[256,2,2048]{2,1,0:T(2,128)} %reshape.220, f32[256,2]{1,0:T(8,128)S(1)} %copy.85), kind=kLoop, calls=%fused_computation.54 | loop fusion | flops 1572864 | bytes 5244928 | tf_op jit(solution)/shard_map/reduce_sum | solution.py:146
  (78 shorter events, 2.6 us)
Async XLA Ops:
  6.5 16.9 %copy-start.3 = (bf16[256,2048]{1,0:T(8,128)(2,1)S(1)}, bf16[256,2048]{1,0:T(8,128)(2,1)}, u32[]{:S(2)}) copy-start(bf16[256,2048]{1,0:T(8,128)(2,1)} %param.10) | copy-start | bytes 3145732
  16.2 14.0 %all-to-all-start = ((bf16[8,96,16]{1,2,0:T(8,128)(2,1)}), bf16[8,96,16]{1,2,0:T(8,128)(2,1)S(1)}, u32[]{:S(2)}, u32[]{:S(2)}) async-start(bf16[8,96,16]{1,2,0:T(8,128)(2,1)} %copy.90), calls=%async_computation | async-start | bytes 65536 | tf_op jit(solution)/shard_map/all_to_all | solution.py:108
  30.2 4.6 %copy-start.4 = (bf16[256,2048]{1,0:T(8,128)(2,1)S(1)}, bf16[256,2048]{1,0:T(8,128)(2,1)}, u32[]{:S(2)}) copy-start(bf16[256,2048]{1,0:T(8,128)(2,1)} %param.11) | copy-start | bytes 3145732
  30.2 74.2 %all-to-all-start.1 = ((bf16[8,96,2048]{2,1,0:T(8,128)(2,1)}), bf16[8,96,2048]{2,1,0:T(8,128)(2,1)}, u32[]{:S(2)}, u32[]{:S(2)}) async-start(bf16[8,96,2048]{2,1,0:T(8,128)(2,1)} %bitcast.146), calls=%async_computation.1 | async-start | bytes 6291456 | tf_op jit(solution)/shard_map/all_to_all | solution.py:106
  104.3 74.5 %all-to-all-start.2 = ((bf16[8,96,2048]{2,1,0:T(8,128)(2,1)}), bf16[8,96,2048]{2,1,0:T(8,128)(2,1)S(1)}, u32[]{:S(2)}, u32[]{:S(2)}) async-start(bf16[8,96,2048]{2,1,0:T(8,128)(2,1)} %bitcast.145), calls=%async_computation.2 | async-start | bytes 6291456 | tf_op jit(solution)/shard_map/all_to_all | solution.py:107
  108.0 160.4 %all-gather.4.cloned.1.call-start = ((), (), s32[]{:S(2)}) async-start(), calls=%async_computation.4 | async-start | bytes 5242880 | tf_op jit(solution)/shard_map/all_gather | solution.py:13
  179.9 2.7 copy-start
  182.5 52.3 %copy-start.6 = (u32[32]{0:T(128)S(1)}, u32[32]{0:T(128)}, u32[]{:S(2)}) copy-start(u32[32]{0:T(128)} %constant.95) | copy-start | bytes 388
  185.5 2.4 copy-start.1
  191.2 3.8 copy-start.2
  202.0 2.4 copy-start.1
  207.7 4.2 %copy-start.2 = (bf16[1,16,256,128]{3,1,2,0:T(8,128)(2,1)S(1)}, bf16[1,16,256,128]{3,1,2,0:T(8,128)(2,1)}, u32[]{:S(2)}) copy-start(bf16[1,16,256,128]{3,1,2,0:T(8,128)(2,1)} %copy-done.1) | copy-start | bytes 3145732 | tf_op jit(solution)/shard_map/while
  219.8 2.4 copy-start.1
  225.5 4.2 %copy-start.2 = (bf16[1,16,256,128]{3,1,2,0:T(8,128)(2,1)S(1)}, bf16[1,16,256,128]{3,1,2,0:T(8,128)(2,1)}, u32[]{:S(2)}) copy-start(bf16[1,16,256,128]{3,1,2,0:T(8,128)(2,1)} %copy-done.1) | copy-start | bytes 3145732 | tf_op jit(solution)/shard_map/while
  286.7 5.9 %copy-start.5 = (f32[256,2]{0,1:T(2,128)S(1)}, f32[256,2]{0,1:T(2,128)}, u32[]{:S(2)}) copy-start(f32[256,2]{0,1:T(2,128)} %param.14) | copy-start | bytes 6148
  286.7 77.9 %all-to-all-start.3 = ((bf16[8,96,2048]{2,1,0:T(8,128)(2,1)}), bf16[8,96,2048]{2,1,0:T(8,128)(2,1)S(1)}, u32[]{:S(2)}, u32[]{:S(2)}) async-start(bf16[8,96,2048]{2,1,0:T(8,128)(2,1)} %reshape.218), calls=%async_computation.3 | async-start | bytes 6291456 | tf_op jit(solution)/shard_map/all_to_all | solution.py:143
Sparse Core Ops, SparseCore 0:
  234.9 33.4 all-gather.3
where the time goes:
time: 397 us; the launch traced here: 390 us
  waiting for transfers between devices  201 us (51%)
  matrix products  68.2 us (17%)
  local copies, waits for them, and re-layouts  59.3 us (15%)
  starting transfers between devices  22 us (6%)
  other arithmetic  18.6 us (5%)
  between operations  14.7 us (4%)
  blocking collectives  5.64 us (1%)
    all_to_all x1, waiting for transfers between devices, on_device(): lax.all_to_all(normed, 'mem', split_axis=0, concat_axis=0, tiled=True)  71.8 us
    all_to_all x1, waiting for transfers between devices, on_device(): lax.all_to_all(send_tokens, 'mem', split_axis=0, concat_axis=0, tiled=True)  65.2 us
    all_to_all x1, waiting for transfers between devices, on_device(): lax.all_to_all(send_queries, 'mem', split_axis=0, concat_axis=0, tiled=True)  44.5 us
    dot_general x1, matrix products, on_device(): jnp.dot(chain_x, kv_weight[0], preferred_element_type=jnp.float32)  17.6 us
    all_gather x1, waiting for transfers between devices, prefix(): gathered = jax.tree.map(lambda a: lax.all_gather(a, axis), part)  17.6 us
    dot_general x3, matrix products, advance(): jnp.einsum('hid,hie->hde', key_block.astype(jnp.float32) * fading[:, :, N...  14.3 us
    dot_general x3, matrix products, advance(): jnp.einsum('hnd,hde->hne', query_block.astype(jnp.float32), carried, prec...  12.2 us
    unnamed x20, local copies, waits for them, and re-layouts  11.8 us
  transfers between devices with their start and end apart: 5, of which 5 were waited for; matrix products, arithmetic and copies ran while one was open for 11% of the time, Pallas kernels for 0%

commit v1 on v0

v1 whole, which is shorter than its diff:
```python
import math

import jax
import jax.numpy as jnp
from jax import lax
from jax.experimental import pallas as pl
from jax.experimental.pallas import tpu as pltpu
from jax.sharding import PartitionSpec as P

F32 = jnp.float32
BF16 = jnp.bfloat16
VMEM_LIMIT = 40 << 20


def mm(a, b):
    return lax.dot_general(a, b, (((1,), (0,)), ((), ())), preferred_element_type=F32)


def mm_nt(a, b):
    return lax.dot_general(a, b, (((1,), (1,)), ((), ())), preferred_element_type=F32)


def split(x):
    high = x.astype(BF16)
    return high, (x - high.astype(F32)).astype(BF16)


def row_slots(routes, members, capacity):
    top, rows = routes.shape
    member = lax.broadcasted_iota(jnp.int32, (members, rows), 0)
    hits = [routes[j : j + 1, :] == member for j in range(top)]
    named = hits[0]
    for h in hits[1:]:
        named = jnp.logical_or(named, h)
    source = lax.broadcasted_iota(jnp.int32, (rows, rows), 0)
    target = lax.broadcasted_iota(jnp.int32, (rows, rows), 1)
    earlier = jnp.where(source < target, 1.0, 0.0).astype(BF16)
    before = mm(jnp.where(named, 1.0, 0.0).astype(BF16), earlier)
    slots = []
    for j in range(top):
        place = jnp.sum(jnp.where(hits[j], before, 0.0), axis=0, keepdims=True)
        slots.append(routes[j : j + 1, :] * capacity + place.astype(jnp.int32))
    return slots


def selection(routes, members, capacity):
    rows = routes.shape[1]
    slots = row_slots(routes, members, capacity)
    index = lax.broadcasted_iota(jnp.int32, (members * capacity, rows), 0)
    chosen = index == slots[0]
    for s in slots[1:]:
        chosen = jnp.logical_or(chosen, index == s)
    return jnp.where(chosen, 1.0, 0.0).astype(BF16)


def dispatch(routes_t, data, members, capacity, parts, decay=None):
    rows, width = data.shape
    chain = members * capacity
    part = width // parts
    tile = min(512, part)
    steps = width // tile
    per = part // tile

    def kernel(*refs):
        if decay is not None:
            routes_ref, data_ref, decay_ref = refs[:3]
            outs, decay_out, pick = refs[3 : 3 + parts], refs[3 + parts], refs[-1]
        else:
            routes_ref, data_ref = refs[:2]
            outs, pick = refs[2 : 2 + parts], refs[-1]
        step = pl.program_id(0)

        @pl.when(step == 0)
        def _():
            chosen = selection(routes_ref[...], members, capacity)
            pick[...] = chosen
            if decay is not None:
                picked = mm_nt(decay_ref[...], chosen).astype(BF16)
                for e in range(members):
                    decay_out[e] = picked[:, e * capacity : (e + 1) * capacity]

        rows_out = mm(pick[...], data_ref[...]).astype(BF16)
        for p in range(parts):

            @pl.when(step // per == p)
            def _():
                outs[p][...] = rows_out

    in_specs = [
        pl.BlockSpec(routes_t.shape, lambda i: (0, 0)),
        pl.BlockSpec((rows, tile), lambda i: (0, i)),
    ]
    args = [routes_t, data]
    out_shape = [jax.ShapeDtypeStruct((chain, part), BF16) for _ in range(parts)]
    out_specs = [
        pl.BlockSpec((chain, tile), lambda i, p=p: (0, jnp.clip(i - p * per, 0, per - 1)))
        for p in range(parts)
    ]
    if decay is not None:
        heads = decay.shape[0]
        in_specs.append(pl.BlockSpec(decay.shape, lambda i: (0, 0)))
        args.append(decay)
        out_shape.append(jax.ShapeDtypeStruct((members, heads, capacity), BF16))
        out_specs.append(pl.BlockSpec((members, heads, capacity), lambda i: (0, 0, 0)))
    return pl.pallas_call(
        kernel,
        grid=(steps,),
        in_specs=in_specs,
        out_specs=out_specs,
        out_shape=out_shape,
        scratch_shapes=[pltpu.VMEM((chain, rows), BF16)],
        compiler_params=pltpu.CompilerParams(vmem_limit_bytes=VMEM_LIMIT),
        cost_estimate=pl.CostEstimate(
            flops=2 * chain * rows * width,
            bytes_accessed=2 * width * (rows + chain),
            transcendentals=0,
        ),
    )(*args)


def local_states(projected, running, head_count, head_size):
    chain = projected.shape[0]

    def kernel(keys_ref, values_ref, running_ref, state_ref):
        h = pl.program_id(0)

        @pl.when(h < head_count)
        def _():
            row = running_ref[pl.ds(h, 1), :]
            fade = jnp.exp(row[:, chain - 1 :] - row)
            faded = keys_ref[...].T.astype(F32) * fade
            high, low = split(faded)
            values = values_ref[...]
            state_ref[0] = mm(high, values) + mm(low, values)

        @pl.when(h == head_count)
        def _():
            state_ref[...] = jnp.zeros_like(state_ref)
            state_ref[0, :head_count, :] = jnp.broadcast_to(
                running_ref[:, chain - 1 :], (head_count, head_size)
            )

    last = head_count - 1
    return pl.pallas_call(
        kernel,
        grid=(head_count + 1,),
        in_specs=[
            pl.BlockSpec((chain, head_size), lambda h: (0, jnp.minimum(h, last))),
            pl.BlockSpec((chain, head_size), lambda h: (0, head_count + jnp.minimum(h, last))),
            pl.BlockSpec(running.shape, lambda h: (0, 0)),
        ],
        out_specs=pl.BlockSpec((1, head_size, head_size), lambda h: (h, 0, 0)),
        out_shape=jax.ShapeDtypeStruct((head_count + 1, head_size, head_size), F32),
        compiler_params=pltpu.CompilerParams(vmem_limit_bytes=VMEM_LIMIT),
        cost_estimate=pl.CostEstimate(
            flops=4 * chain * head_size * head_size * head_count,
            bytes_accessed=projected.size * 2 + head_count * head_size * head_size * 4,
            transcendentals=chain * head_count,
        ),
    )(projected, projected, running)


def chain_outputs(queries, projected, running, incoming, first_head, head_count, head_size, rows):
    chain, width = queries.shape
    here = width // head_size

    def kernel(queries_ref, keys_ref, values_ref, running_ref, incoming_ref, out_ref):
        h = pl.program_id(0) + first_head
        state = incoming_ref[0]
        running_row = running_ref[pl.ds(h, 1), :]
        up = lax.broadcasted_iota(jnp.int32, (rows, rows), 0)
        across = lax.broadcasted_iota(jnp.int32, (rows, rows), 1)
        lower = up >= across
        previous = jnp.zeros((1, 1), F32)
        for c in range(chain // rows):
            span = slice(c * rows, (c + 1) * rows)
            query, key, value = queries_ref[span, :], keys_ref[span, :], values_ref[span, :]
            row = running_row[:, span]
            wide = jnp.broadcast_to(row, (rows, rows))
            tall = wide.T
            weights = jnp.where(lower, jnp.exp(jnp.minimum(tall - wide, 0.0)), 0.0)
            scores, scores_low = split(mm_nt(query, key) * weights)
            state_high, state_low = split(state)
            grown = jnp.exp(tall[:, :head_size] - previous)
            earlier = (mm(query, state_high) + mm(query, state_low)) * grown
            outputs = mm(scores, value) + mm(scores_low, value) + earlier
            mean_square = jnp.mean(outputs * outputs, axis=-1, keepdims=True)
            out_ref[span, :] = (outputs * lax.rsqrt(mean_square + 1e-06)).astype(BF16)
            ending = row[:, rows - 1 :]
            if (c + 1) * rows < chain:
                faded, faded_low = split(key.T.astype(F32) * jnp.exp(ending - row))
                state = (
                    jnp.exp(ending - previous) * state + mm(faded, value) + mm(faded_low, value)
                )
            previous = ending

    return pl.pallas_call(
        kernel,
        grid=(here,),
        in_specs=[
            pl.BlockSpec((chain, head_size), lambda h: (0, h)),
            pl.BlockSpec((chain, head_size), lambda h: (0, first_head + h)),
            pl.BlockSpec((chain, head_size), lambda h: (0, head_count + first_head + h)),
            pl.BlockSpec(running.shape, lambda h: (0, 0)),
            pl.BlockSpec((1, head_size, head_size), lambda h: (first_head + h, 0, 0)),
        ],
        out_specs=pl.BlockSpec((chain, head_size), lambda h: (0, h)),
        out_shape=jax.ShapeDtypeStruct((chain, width), BF16),
        compiler_params=pltpu.CompilerParams(vmem_limit_bytes=VMEM_LIMIT),
        cost_estimate=pl.CostEstimate(
            flops=here * chain * head_size * (6 * rows + 8 * head_size),
            bytes_accessed=8 * chain * width,
            transcendentals=here * chain * rows,
        ),
    )(queries, projected, projected, running, incoming)


def combine(route_ids, gate_weights, returned, mixed, part, parts, members, capacity):
    rows, top = route_ids.shape
    chain, width = returned.shape
    tile = min(512, width)
    steps = width // tile

    def kernel(*refs):
        routes_ref, gates_ref, returned_ref = refs[:3]
        out_ref, high_ref, low_ref = refs[-3:]

        @pl.when(pl.program_id(0) == 0)
        def _():
            routes = routes_ref[...]
            member = lax.broadcasted_iota(jnp.int32, (rows, members), 1)
            hits = [routes[:, j : j + 1] == member for j in range(top)]
            named = hits[0]
            for hit in hits[1:]:
                named = jnp.logical_or(named, hit)
            target = lax.broadcasted_iota(jnp.int32, (rows, rows), 0)
            source = lax.broadcasted_iota(jnp.int32, (rows, rows), 1)
            earlier = jnp.where(source < target, 1.0, 0.0).astype(BF16)
            before = mm(earlier, jnp.where(named, 1.0, 0.0).astype(BF16))
            index = lax.broadcasted_iota(jnp.int32, (rows, chain), 1)
            gates = jnp.zeros((rows, chain), F32)
            for j in range(top):
                place = jnp.sum(jnp.where(hits[j], before, 0.0), axis=1, keepdims=True)
                slot = routes[:, j : j + 1] * capacity + place.astype(jnp.int32)
                gates = jnp.where(index == slot, gates_ref[:, j : j + 1], gates)
            high_ref[...], low_ref[...] = split(gates)

        data = returned_ref[...]
        out_ref[...] = (mm(high_ref[...], data) + mm(low_ref[...], data)).astype(BF16)

    in_specs = [
        pl.BlockSpec((rows, top), lambda i: (0, 0)),
        pl.BlockSpec((rows, top), lambda i: (0, 0)),
        pl.BlockSpec((chain, tile), lambda i: (0, i)),
    ]
    args = [route_ids, gate_weights, returned]
    aliases = {}
    if mixed is not None:
        in_specs.append(pl.BlockSpec(memory_space=pl.ANY))
        args.append(mixed)
        aliases = {3: 0}
    return pl.pallas_call(
        kernel,
        grid=(steps,),
        in_specs=in_specs,
        out_specs=pl.BlockSpec((rows, tile), lambda i: (0, part * steps + i)),
        out_shape=jax.ShapeDtypeStruct((rows, width * parts), BF16),
        scratch_shapes=[pltpu.VMEM((rows, chain), BF16), pltpu.VMEM((rows, chain), BF16)],
        input_output_aliases=aliases,
        compiler_params=pltpu.CompilerParams(vmem_limit_bytes=VMEM_LIMIT),
        cost_estimate=pl.CostEstimate(
            flops=4 * rows * chain * width,
            bytes_accessed=2 * width * (rows + chain),
            transcendentals=0,
        ),
    )(*args)


def earlier_state(states, axis, head_count):
    size = lax.axis_size(axis)
    place = lax.axis_index(axis)
    total, total_log = states[:head_count], states[head_count, :head_count, 0]
    found = jnp.zeros_like(total)
    found_log = jnp.zeros_like(total_log)
    step = 1
    while step < size:
        last = step * 2 >= size
        if last:
            pairs = [(i, i + step) for i in range(size - step) if not i & step]
        else:
            pairs = [(i, i ^ step) for i in range(size)]
        planes = jnp.concatenate(
            [total, jnp.zeros((1,) + total.shape[1:], F32).at[0, :head_count, :].set(total_log[:, None])]
        ) if step > 1 else states
        other = lax.ppermute(planes, axis, pairs)
        other_total, other_log = other[:head_count], other[head_count, :head_count, 0]
        upper = (place & step) != 0
        found = found + jnp.where(upper, jnp.exp(found_log), 0.0)[:, None, None] * other_total
        found_log = found_log + jnp.where(upper, other_log, 0.0)
        if not last:
            mine = jnp.where(upper, 1.0, jnp.exp(other_log))[:, None, None]
            theirs = jnp.where(upper, jnp.exp(total_log), 1.0)[:, None, None]
            total = mine * total + theirs * other_total
            total_log = total_log + other_log
        step *= 2
    return found


def on_device(tokens, queries, log_decay, route_ids, gate_weights, kv_weight):
    tok_rows, model_width = tokens.shape
    head_count = log_decay.shape[1]
    head_size = model_width // head_count
    top_count = route_ids.shape[1]
    members = lax.axis_size("mem")
    capacity = 3 * tok_rows * top_count // (2 * members)
    chain_rows = members * capacity
    parts = 2
    routes_t = route_ids.T
    decay_t = log_decay.T

    def swap(rows):
        sent = rows.reshape(members, capacity, rows.shape[-1])
        return lax.all_to_all(sent, "mem", split_axis=0, concat_axis=0, tiled=True).reshape(
            rows.shape
        )

    send_tokens, send_decay = dispatch(routes_t, tokens, members, capacity, 1, decay_t)
    received_decay = lax.all_to_all(send_decay, "mem", split_axis=0, concat_axis=0, tiled=True)
    chain_x = swap(send_tokens)
    send_queries = dispatch(routes_t, queries, members, capacity, parts)
    query_parts = [swap(q) for q in send_queries]
    logs = jnp.moveaxis(received_decay, 0, 1).reshape(head_count, chain_rows).astype(F32)
    running = jnp.cumsum(logs, axis=1)
    projected = jnp.dot(chain_x, kv_weight[0], preferred_element_type=F32).astype(BF16)
    states = local_states(projected, running, head_count, head_size)
    incoming = earlier_state(states, "tm", head_count)
    rows = math.gcd(chain_rows, 128)
    heads_part = head_count // parts
    mixed = None
    for p in range(parts):
        normed = chain_outputs(
            query_parts[p], projected, running, incoming, p * heads_part, head_count, head_size, rows
        )
        mixed = combine(
            route_ids, gate_weights, swap(normed), mixed, p, parts, members, capacity
        )
    return mixed


def solution(mesh):
    placed = (
        P(("tm", "mem"), None),
        P(("tm", "mem"), None),
        P(("tm", "mem"), None),
        P(("tm", "mem"), None),
        P(("tm", "mem"), None),
        P("mem", None, None),
    )
    return jax.shard_map(
        on_device, mesh=mesh, in_specs=placed, out_specs=P(("tm", "mem"), None), check_vma=False
    )
```

time: 397 us -> 273 us (0.69); the launches traced: 390 us -> 273 us
  waiting for transfers between devices: 201 us -> 150 us
  matrix products: 68.2 us -> 17.6 us
  local copies, waits for them, and re-layouts: 59.3 us -> 12.3 us
  Pallas kernels: 0 us -> 46.9 us
  between operations: 14.7 us -> 0.21 us
  other arithmetic: 18.6 us -> 5.89 us
  blocking collectives: 5.64 us -> 13.8 us
  starting transfers between devices: 22 us -> 26.4 us
    all_to_all x4 -> x5, waiting for transfers between devices: 184 us -> 127 us  [swap(): lax.all_to_all(sent, 'mem', split_axis=0, concat_axis=0, tiled=True)]
    dot_general x14 -> x1, matrix products: 68.2 us -> 17.6 us  [on_device(): jnp.dot(chain_x, kv_weight[0], preferred_element_type=F32).astype(BF16)]
    pallas_call x0 -> x7, Pallas kernels: none -> 46.9 us  [the longest x2 26.4 us: chain_outputs(): pl.pallas_call(kernel, grid=(here,), in_specs=[pl.BlockSpec((chain, head_...]
    ppermute x0 -> x2, waiting for transfers between devices: none -> 22 us  [earlier_state(): other = lax.ppermute(planes, axis, pairs)]
    all_gather x1 -> x0, waiting for transfers between devices: 17.6 us -> none  [prefix(): gathered = jax.tree.map(lambda a: lax.all_gather(a, axis), part)]
    gather x4 -> x0, local copies, waits for them, and re-layouts: 13.9 us -> none  [the longest x1 4.37 us: on_device(): padded_tokens[slot_token].reshape(members, capacity, model_width)]
    all_to_all x0 -> x1, blocking collectives: none -> 13.8 us  [on_device(): lax.all_to_all(send_decay, 'mem', split_axis=0, concat_axis=0, tiled=True)]
    reshape x8 -> x0, local copies, waits for them, and re-layouts: 13.4 us -> none  [the longest x1 6.61 us: block_pass(): jnp.moveaxis(outputs, 0, 1).reshape(head_count, chain_rows, head_size)]
  transfers between devices with their start and end apart: 5 -> 7, of which waited for: 5 -> 5; matrix products, arithmetic and copies ran while one was open for 11% -> 9% of each run, Pallas kernels for 0% -> 15%
where the time goes in v1:
time: 273 us
  waiting for transfers between devices  150 us (55%)
  Pallas kernels  46.9 us (17%)
  starting transfers between devices  26.4 us (10%)
  matrix products  17.6 us (6%)
  blocking collectives  13.8 us (5%)
  local copies, waits for them, and re-layouts  12.3 us (5%)
  other arithmetic  5.89 us (2%)
    all_to_all x5, waiting for transfers between devices, swap(): lax.all_to_all(sent, 'mem', split_axis=0, concat_axis=0, tiled=True)  127 us
    pallas_call x2, Pallas kernels, chain_outputs(): pl.pallas_call(kernel, grid=(here,), in_specs=[pl.BlockSpec((chain, head_...  26.4 us
    ppermute x2, waiting for transfers between devices, earlier_state(): other = lax.ppermute(planes, axis, pairs)  22 us
    all_to_all x5, starting transfers between devices, swap(): lax.all_to_all(sent, 'mem', split_axis=0, concat_axis=0, tiled=True)  21.9 us
    dot_general x1, matrix products, on_device(): jnp.dot(chain_x, kv_weight[0], preferred_element_type=F32).astype(BF16)  17.6 us
    all_to_all x1, blocking collectives, on_device(): lax.all_to_all(send_decay, 'mem', split_axis=0, concat_axis=0, tiled=True)  13.8 us
    unnamed x28, local copies, waits for them, and re-layouts  11.9 us
    pallas_call x2, Pallas kernels, dispatch(): pl.pallas_call(kernel, grid=(steps,), in_specs=in_specs, out_specs=out_sp...  7.63 us
  transfers between devices with their start and end apart: 7, of which 5 were waited for; matrix products, arithmetic and copies ran while one was open for 9% of the time, Pallas kernels for 15%

profile of v1, /device:TPU:0, one launch (start us, length us, event | category | flops | bytes accessed | tf_op | source)
XLA Modules:
  0.0 272.6 jit_solution(9991034503490741921)
XLA Ops:
  0.0 0.0 copy-start.7
  0.0 0.7 copy-done.7
  0.7 0.0 copy-start.9
  0.7 1.2 copy-done.9
  1.9 0.0 copy-start.11
  1.9 0.7 copy-done.11
  2.6 3.8 %shard_map.65 = (bf16[768,2048]{1,0:T(8,128)(2,1)}, bf16[8,16,96]{2,1,0:T(8,128)(2,1)S(1)}) custom-call(s32[2,256]{1,0:T(2,128)S(1)} %bitcast.31, bf16[256,2048]{1,0:T(8,128)(2,1)S(1)} %copy-done.9, bf16[16,256]{1,0:T(8,128)(2,1)S(1)} %bitcast.33), custom_call_target="tpu_custom_call" | custom-call | flops 805306368 | bytes 4194304 | tf_op jit(solution)/shard_map/pallas_call | solution.py:105
  6.4 13.8 %all_to_all.30 = bf16[8,16,96]{2,1,0:T(8,128)(2,1)S(1)} all-to-all(bf16[8,16,96]{2,1,0:T(8,128)(2,1)S(1)} %get-tuple-element.23), channel_id=1, replica_groups=mesh['tm'=4,'mem'=8] {'mem'}, dimensions={0} | all-to-all | bytes 49152 | tf_op jit(solution)/shard_map/all_to_all | solution.py:328
  20.2 0.0 copy-start.8
  20.2 0.0 copy-start.10
  20.2 4.6 %all-to-all-start.1 = ((bf16[8,96,2048]{2,1,0:T(8,128)(2,1)}), bf16[8,96,2048]{2,1,0:T(8,128)(2,1)}, u32[]{:S(2)}, u32[]{:S(2)}) async-start(bf16[8,96,2048]{2,1,0:T(8,128)(2,1)} %bitcast.4), calls=%async_computation.1 | async-start | bytes 6291456 | tf_op jit(solution)/shard_map/all_to_all | solution.py:323
  24.8 0.0 copy-done.8
  24.8 0.0 copy-done.10
  24.8 3.8 %shard_map.64 = (bf16[768,1024]{1,0:T(8,128)(2,1)}, bf16[768,1024]{1,0:T(8,128)(2,1)S(1)}) custom-call(s32[2,256]{1,0:T(2,128)S(1)} %bitcast.32, bf16[256,2048]{1,0:T(8,128)(2,1)S(1)} %copy-done.10), custom_call_target="tpu_custom_call" | custom-call | flops 805306368 | bytes 4194304 | tf_op jit(solution)/shard_map/pallas_call | solution.py:105
  28.6 0.0 copy-start.4
  28.6 1.1 copy-done.4
  29.8 0.1 reshape.139
  29.9 1.7 reduce-window.6
  31.6 0.2 slice_reduce_fusion
  31.8 0.1 copy_bitcast_fusion.running_ref
  31.9 62.5 %all-to-all-done.1 = bf16[8,96,2048]{2,1,0:T(8,128)(2,1)} async-done(((bf16[8,96,2048]{2,1,0:T(8,128)(2,1)}), bf16[8,96,2048]{2,1,0:T(8,128)(2,1)}, u32[]{:S(2)}, u32[]{:S(2)}) %all-to-all-start.1) | async-done | bytes 3145760 | tf_op jit(solution)/shard_map/all_to_all | solution.py:323
  94.4 3.6 %all-to-all-start.4 = ((bf16[8,96,1024]{2,1,0:T(8,128)(2,1)}), bf16[8,96,1024]{2,1,0:T(8,128)(2,1)S(1)}, u32[]{:S(2)}, u32[]{:S(2)}) async-start(bf16[8,96,1024]{2,1,0:T(8,128)(2,1)} %bitcast.10), calls=%async_computation.4 | async-start | bytes 3145728 | tf_op jit(solution)/shard_map/all_to_all | solution.py:323
  98.0 17.6 %fusion.2.keys_ref.values_ref = bf16[768,4096]{1,0:T(8,128)(2,1)S(1)} fusion(bf16[768,2048]{1,0:T(8,128)(2,1)} %bitcast.5, bf16[1,2048,4096]{2,1,0:T(8,128)(2,1)} %param.13), kind=kOutput, calls=%fused_computation.2 | convolution fusion | flops 12888047616 | bytes 26214400 | tf_op jit(solution)/shard_map/dot_general | solution.py:334
  115.6 0.0 copy-start
  115.6 7.5 %shard_map.66 = f32[17,128,128]{2,1,0:T(8,128)S(1)} custom-call(bf16[768,4096]{1,0:T(8,128)(2,1)S(1)} %fusion.2.keys_ref.values_ref, bf16[768,4096]{1,0:T(8,128)(2,1)S(1)} %fusion.2.keys_ref.values_ref, f32[16,768]{1,0:T(8,128)S(1)} %copy_bitcast_fusion.running_ref), custom_call_target="tpu_custom_call" | custom-call | flops 805306368 | bytes 7340032 | tf_op jit(solution)/shard_map/pallas_call | solution.py:144
  123.2 0.0 copy-done
  123.2 0.1 collective-permute-start
  123.2 11.9 %all-to-all-done.4 = bf16[8,96,1024]{2,1,0:T(8,128)(2,1)S(1)} async-done(((bf16[8,96,1024]{2,1,0:T(8,128)(2,1)}), bf16[8,96,1024]{2,1,0:T(8,128)(2,1)S(1)}, u32[]{:S(2)}, u32[]{:S(2)}) %all-to-all-start.4) | async-done | bytes 1572896 | tf_op jit(solution)/shard_map/all_to_all | solution.py:323
  135.2 4.3 %all-to-all-start = ((bf16[8,96,1024]{2,1,0:T(8,128)(2,1)}), bf16[8,96,1024]{2,1,0:T(8,128)(2,1)}, u32[]{:S(2)}, u32[]{:S(2)}) async-start(bf16[8,96,1024]{2,1,0:T(8,128)(2,1)} %bitcast.29), calls=%async_computation | async-start | bytes 3145728 | tf_op jit(solution)/shard_map/all_to_all | solution.py:323
  139.5 0.0 collective-permute-done
  139.5 0.9 select_reduce_fusion.2
  140.4 1.4 fusion.6
  141.8 0.1 scatter.8
  141.9 0.1 pad_maximum_fusion
  141.9 4.4 %collective-permute-start.1 = (f32[17,128,128]{2,1,0:T(8,128)S(1)}, f32[17,128,128]{2,1,0:T(8,128)}, u32[]{:S(2)}, u32[]{:S(2)}) collective-permute-start(f32[17,128,128]{2,1,0:T(8,128)S(1)} %pad_maximum_fusion), channel_id=1, source_target_pairs={{0,16},{8,24},{1,17},{9,25},{2,18},{10,26},{3,19},{11,27},{4,20},{... | collective-permute-start | bytes 3342344 | tf_op jit(solution)/shard_map/ppermute | solution.py:295
  146.4 22.0 %collective-permute-done.1 = f32[17,128,128]{2,1,0:T(8,128)} collective-permute-done((f32[17,128,128]{2,1,0:T(8,128)S(1)}, f32[17,128,128]{2,1,0:T(8,128)}, u32[]{:S(2)}, u32[]{:S(2)}) %collective-permute-start.1) | collective-permute-done | bytes 1114144 | tf_op jit(solution)/shard_map/ppermute | solution.py:295
  168.4 1.7 fusion.5.incoming_ref
  170.1 0.0 copy-start.1
  170.1 2.8 %copy-done.1 = bf16[768,4096]{1,0:T(8,128)(2,1)S(1)} copy-done((bf16[768,4096]{1,0:T(8,128)(2,1)S(1)}, bf16[768,4096]{1,0:T(8,128)(2,1)}, u32[]{:S(2)}) %copy-start.1) | copy-done | bytes 6291480
  172.9 12.8 %shard_map.68 = bf16[768,1024]{1,0:T(8,128)(2,1)S(1)} custom-call(bf16[768,1024]{1,0:T(8,128)(2,1)S(1)} %bitcast.26, bf16[768,4096]{1,0:T(8,128)(2,1)S(1)} %copy-done.1, bf16[768,4096]{1,0:T(8,128)(2,1)S(1)} %copy-done.1, f32[16,768]{1,0:T(8,128)S(1)} %copy_bitcast_fusion.running_ref, f32[16,128,128]{2,1,0:T(8,128)S(1)} %fusion.5.incoming_ref), custom_call_target="tpu_custom_call" | custom-call | flops 1409286144 | bytes 6291456 | tf_op jit(solution)/shard_map/pallas_call | solution.py:197
  185.7 0.0 copy-start.3
  185.7 1.2 copy-done.3
  186.9 0.0 all-to-all-done
  186.9 5.7 %all-to-all-start.5 = ((bf16[8,96,1024]{2,1,0:T(8,128)(2,1)}), bf16[8,96,1024]{2,1,0:T(8,128)(2,1)S(1)}, u32[]{:S(2)}, u32[]{:S(2)}) async-start(bf16[8,96,1024]{2,1,0:T(8,128)(2,1)} %bitcast.27), calls=%async_computation.5 | async-start | bytes 3145728 | tf_op jit(solution)/shard_map/all_to_all | solution.py:323
  192.6 0.0 copy-start.2
  192.6 2.8 %copy-done.2 = bf16[768,4096]{1,0:T(8,128)(2,1)S(1)} copy-done((bf16[768,4096]{1,0:T(8,128)(2,1)S(1)}, bf16[768,4096]{1,0:T(8,128)(2,1)}, u32[]{:S(2)}) %copy-start.2) | copy-done | bytes 6291480
  195.4 13.6 %shard_map.67 = bf16[768,1024]{1,0:T(8,128)(2,1)} custom-call(bf16[768,1024]{1,0:T(8,128)(2,1)} %bitcast.2.queries_ref, bf16[768,4096]{1,0:T(8,128)(2,1)S(1)} %copy-done.2, bf16[768,4096]{1,0:T(8,128)(2,1)S(1)} %copy-done.2, f32[16,768]{1,0:T(8,128)S(1)} %copy_bitcast_fusion.running_ref, f32[16,128,128]{2,1,0:T(8,128)S(1)} %fusion.5.incoming_ref), custom_call_target="tpu_custom_call" | custom-call | flops 1409286144 | bytes 6291456 | tf_op jit(solution)/shard_map/pallas_call | solution.py:197
  208.9 19.1 %all-to-all-done.5 = bf16[8,96,1024]{2,1,0:T(8,128)(2,1)S(1)} async-done(((bf16[8,96,1024]{2,1,0:T(8,128)(2,1)}), bf16[8,96,1024]{2,1,0:T(8,128)(2,1)S(1)}, u32[]{:S(2)}, u32[]{:S(2)}) %all-to-all-start.5) | async-done | bytes 1572896 | tf_op jit(solution)/shard_map/all_to_all | solution.py:323
  228.0 0.0 copy-start.5
  228.0 1.2 copy-done.5
  229.2 0.0 copy-start.12
  229.2 0.0 copy-start.6
  229.2 3.7 %all-to-all-start.3 = ((bf16[8,96,1024]{2,1,0:T(8,128)(2,1)}), bf16[8,96,1024]{2,1,0:T(8,128)(2,1)S(1)}, u32[]{:S(2)}, u32[]{:S(2)}) async-start(bf16[8,96,1024]{2,1,0:T(8,128)(2,1)} %bitcast.8), calls=%async_computation.3 | async-start | bytes 3145728 | tf_op jit(solution)/shard_map/all_to_all | solution.py:323
  232.9 0.1 copy.18.refs_0_
  233.0 0.0 copy-done.12
  233.0 0.1 copy.19.refs_1_
  233.2 0.0 copy-done.6
  233.2 2.7 shard_map.69.refs_3_
  235.9 34.0 %all-to-all-done.3 = bf16[8,96,1024]{2,1,0:T(8,128)(2,1)S(1)} async-done(((bf16[8,96,1024]{2,1,0:T(8,128)(2,1)}), bf16[8,96,1024]{2,1,0:T(8,128)(2,1)S(1)}, u32[]{:S(2)}, u32[]{:S(2)}) %all-to-all-start.3) | async-done | bytes 1572896 | tf_op jit(solution)/shard_map/all_to_all | solution.py:323
  269.9 2.7 shard_map.70
  (5 shorter events, 0.1 us)
Async XLA Ops:
  0.0 0.7 copy-start.7
  0.7 1.2 copy-start.9
  1.9 0.7 copy-start.11
  20.2 4.6 %copy-start.8 = (s32[256,2]{0,1:T(2,128)S(1)}, s32[256,2]{0,1:T(2,128)}, u32[]{:S(2)}) copy-start(s32[256,2]{0,1:T(2,128)} %param.11) | copy-start | bytes 6148
  20.2 4.6 %copy-start.10 = (bf16[256,2048]{1,0:T(8,128)(2,1)S(1)}, bf16[256,2048]{1,0:T(8,128)(2,1)}, u32[]{:S(2)}) copy-start(bf16[256,2048]{1,0:T(8,128)(2,1)} %refs_1_.4) | copy-start | bytes 3145732
  20.2 74.1 %all-to-all-start.1 = ((bf16[8,96,2048]{2,1,0:T(8,128)(2,1)}), bf16[8,96,2048]{2,1,0:T(8,128)(2,1)}, u32[]{:S(2)}, u32[]{:S(2)}) async-start(bf16[8,96,2048]{2,1,0:T(8,128)(2,1)} %bitcast.4), calls=%async_computation.1 | async-start | bytes 6291456 | tf_op jit(solution)/shard_map/all_to_all | solution.py:323
  28.6 1.1 copy-start.4
  94.4 40.8 %all-to-all-start.4 = ((bf16[8,96,1024]{2,1,0:T(8,128)(2,1)}), bf16[8,96,1024]{2,1,0:T(8,128)(2,1)S(1)}, u32[]{:S(2)}, u32[]{:S(2)}) async-start(bf16[8,96,1024]{2,1,0:T(8,128)(2,1)} %bitcast.10), calls=%async_computation.4 | async-start | bytes 3145728 | tf_op jit(solution)/shard_map/all_to_all | solution.py:323
  115.6 7.6 %copy-start = (bf16[768,4096]{1,0:T(8,128)(2,1)}, bf16[768,4096]{1,0:T(8,128)(2,1)S(1)}, u32[]{:S(2)}) copy-start(bf16[768,4096]{1,0:T(8,128)(2,1)S(1)} %fusion.2.keys_ref.values_ref) | copy-start | bytes 18874372
  123.2 16.3 %collective-permute-start = (f32[17,128,128]{2,1,0:T(8,128)S(1)}, f32[17,128,128]{2,1,0:T(8,128)}, u32[]{:S(2)}, u32[]{:S(2)}) collective-permute-start(f32[17,128,128]{2,1,0:T(8,128)S(1)} %shard_map.66), channel_id=1, source_target_pairs={{0,8},{8,0},{16,24},{24,16},{1,9},{9,1},{17,25},{25,17},{2,10},{10... | collective-permute-start | bytes 3342344 | tf_op jit(solution)/shard_map/ppermute | solution.py:295
  135.2 51.7 %all-to-all-start = ((bf16[8,96,1024]{2,1,0:T(8,128)(2,1)}), bf16[8,96,1024]{2,1,0:T(8,128)(2,1)}, u32[]{:S(2)}, u32[]{:S(2)}) async-start(bf16[8,96,1024]{2,1,0:T(8,128)(2,1)} %bitcast.29), calls=%async_computation | async-start | bytes 3145728 | tf_op jit(solution)/shard_map/all_to_all | solution.py:323
  141.9 26.4 %collective-permute-start.1 = (f32[17,128,128]{2,1,0:T(8,128)S(1)}, f32[17,128,128]{2,1,0:T(8,128)}, u32[]{:S(2)}, u32[]{:S(2)}) collective-permute-start(f32[17,128,128]{2,1,0:T(8,128)S(1)} %pad_maximum_fusion), channel_id=1, source_target_pairs={{0,16},{8,24},{1,17},{9,25},{2,18},{10,26},{3,19},{11,27},{4,20},{... | collective-permute-start | bytes 3342344 | tf_op jit(solution)/shard_map/ppermute | solution.py:295
  170.1 2.8 %copy-start.1 = (bf16[768,4096]{1,0:T(8,128)(2,1)S(1)}, bf16[768,4096]{1,0:T(8,128)(2,1)}, u32[]{:S(2)}) copy-start(bf16[768,4096]{1,0:T(8,128)(2,1)} %copy-done) | copy-start | bytes 18874372
  185.7 1.2 copy-start.3
  186.9 41.1 %all-to-all-start.5 = ((bf16[8,96,1024]{2,1,0:T(8,128)(2,1)}), bf16[8,96,1024]{2,1,0:T(8,128)(2,1)S(1)}, u32[]{:S(2)}, u32[]{:S(2)}) async-start(bf16[8,96,1024]{2,1,0:T(8,128)(2,1)} %bitcast.27), calls=%async_computation.5 | async-start | bytes 3145728 | tf_op jit(solution)/shard_map/all_to_all | solution.py:323
  192.6 2.8 %copy-start.2 = (bf16[768,4096]{1,0:T(8,128)(2,1)S(1)}, bf16[768,4096]{1,0:T(8,128)(2,1)}, u32[]{:S(2)}) copy-start(bf16[768,4096]{1,0:T(8,128)(2,1)} %copy-done) | copy-start | bytes 18874372
  228.0 1.2 copy-start.5
  229.2 3.9 %copy-start.12 = (f32[256,2]{0,1:T(2,128)S(1)}, f32[256,2]{0,1:T(2,128)}, u32[]{:S(2)}) copy-start(f32[256,2]{0,1:T(2,128)} %param.12) | copy-start | bytes 6148
  229.2 4.0 %copy-start.6 = (bf16[8,96,1024]{2,1,0:T(8,128)(2,1)S(1)}, bf16[8,96,1024]{2,1,0:T(8,128)(2,1)}, u32[]{:S(2)}) copy-start(bf16[8,96,1024]{2,1,0:T(8,128)(2,1)} %copy-done.5) | copy-start | bytes 4718596
  229.2 40.7 %all-to-all-start.3 = ((bf16[8,96,1024]{2,1,0:T(8,128)(2,1)}), bf16[8,96,1024]{2,1,0:T(8,128)(2,1)S(1)}, u32[]{:S(2)}, u32[]{:S(2)}) async-start(bf16[8,96,1024]{2,1,0:T(8,128)(2,1)} %bitcast.8), calls=%async_computation.3 | async-start | bytes 3145728 | tf_op jit(solution)/shard_map/all_to_all | solution.py:323

commit v2 on v1

v2 whole, which is shorter than its diff:
```python
import math

import jax
import jax.numpy as jnp
from jax import lax
from jax.experimental import pallas as pl
from jax.experimental.pallas import tpu as pltpu
from jax.sharding import PartitionSpec as P

F32 = jnp.float32
BF16 = jnp.bfloat16
VMEM_LIMIT = 40 << 20
LANES = 128
FACT_PAD = 4
HEAD_PARTS = (8, 8)


def mm(a, b):
    return lax.dot_general(a, b, (((1,), (0,)), ((), ())), preferred_element_type=F32)


def mm_nt(a, b):
    return lax.dot_general(a, b, (((1,), (1,)), ((), ())), preferred_element_type=F32)


def split(x):
    high = x.astype(BF16)
    return high, (x - high.astype(F32)).astype(BF16)


def row_slots(routes, members, capacity):
    top, rows = routes.shape
    member = lax.broadcasted_iota(jnp.int32, (members, rows), 0)
    hits = [routes[j : j + 1, :] == member for j in range(top)]
    named = hits[0]
    for hit in hits[1:]:
        named = jnp.logical_or(named, hit)
    source = lax.broadcasted_iota(jnp.int32, (rows, rows), 0)
    target = lax.broadcasted_iota(jnp.int32, (rows, rows), 1)
    earlier = jnp.where(source < target, 1.0, 0.0).astype(BF16)
    before = mm(jnp.where(named, 1.0, 0.0).astype(BF16), earlier)
    slots = []
    for j in range(top):
        place = jnp.sum(jnp.where(hits[j], before, 0.0), axis=0, keepdims=True)
        slots.append(routes[j : j + 1, :] * capacity + place.astype(jnp.int32))
    return slots


def half_slots(facts, half, top, members, capacity):
    rows = facts.shape[1]
    share = members // 2 * capacity
    slots = row_slots(facts[:top, :].astype(jnp.int32), members, capacity)
    index = lax.broadcasted_iota(jnp.int32, (share, rows), 0) + half * share
    return slots, index


SMEM_SPEC = pl.BlockSpec(memory_space=pltpu.SMEM)
VMEM_SPEC = pl.BlockSpec(memory_space=pltpu.VMEM)


def dispatch(half, facts, data, top, members, capacity, heads):
    rows, width = data.shape
    share = members // 2 * capacity
    full = width + (LANES if heads else 0)
    tile = 512

    def kernel(half_ref, facts_ref, data_ref, out_ref):
        slots, index = half_slots(facts_ref[...], half_ref[0], top, members, capacity)
        chosen = index == slots[0]
        for slot in slots[1:]:
            chosen = jnp.logical_or(chosen, index == slot)
        pick = jnp.where(chosen, 1.0, 0.0).astype(BF16)
        for c in range(0, width, tile):
            out_ref[:, c : c + tile] = mm(pick, data_ref[:, c : c + tile]).astype(BF16)
        if heads:
            decay = facts_ref[2 * top + FACT_PAD :, :].astype(BF16)
            decay = jnp.concatenate([decay, jnp.zeros((LANES - heads, rows), BF16)], axis=0)
            out_ref[:, width:] = mm_nt(pick, decay).astype(BF16)

    return pl.pallas_call(
        kernel,
        in_specs=[SMEM_SPEC, VMEM_SPEC, VMEM_SPEC],
        out_specs=VMEM_SPEC,
        out_shape=jax.ShapeDtypeStruct((share, full), BF16),
        compiler_params=pltpu.CompilerParams(vmem_limit_bytes=VMEM_LIMIT),
        cost_estimate=pl.CostEstimate(
            flops=2 * share * rows * width,
            bytes_accessed=2 * width * (rows + share),
            transcendentals=0,
        ),
    )(half, facts, data)


def gate_matrices(half, facts, partner_facts, top, members, capacity):
    rows = facts.shape[1]
    share = members // 2 * capacity

    def kernel(half_ref, facts_ref, partner_ref, high_ref, low_ref):
        for b, ref in enumerate((facts_ref, partner_ref)):
            values = ref[...]
            slots, index = half_slots(values, half_ref[0], top, members, capacity)
            gates = jnp.zeros((share, rows), F32)
            for j in range(top):
                gates = jnp.where(index == slots[j], values[top + j : top + j + 1, :], gates)
            high_ref[b], low_ref[b] = split(gates.T)

    shape = jax.ShapeDtypeStruct((2, rows, share), BF16)
    return pl.pallas_call(
        kernel,
        in_specs=[SMEM_SPEC, VMEM_SPEC, VMEM_SPEC],
        out_specs=[VMEM_SPEC, VMEM_SPEC],
        out_shape=[shape, shape],
        compiler_params=pltpu.CompilerParams(vmem_limit_bytes=VMEM_LIMIT),
        cost_estimate=pl.CostEstimate(
            flops=4 * rows * rows * members,
            bytes_accessed=8 * rows * share,
            transcendentals=0,
        ),
    )(half, facts, partner_facts)


def project(rows_in, weight):
    share = rows_in.shape[0]
    depth, width = weight.shape
    tile = 512

    def kernel(rows_ref, weight_ref, out_ref):
        out_ref[...] = mm(rows_ref[...], weight_ref[...]).astype(BF16)

    return pl.pallas_call(
        kernel,
        grid=(width // tile,),
        in_specs=[
            pl.BlockSpec((share, depth), lambda i: (0, 0)),
            pl.BlockSpec((depth, tile), lambda i: (0, i)),
        ],
        out_specs=pl.BlockSpec((share, tile), lambda i: (0, i)),
        out_shape=jax.ShapeDtypeStruct((share, width), BF16),
        compiler_params=pltpu.CompilerParams(vmem_limit_bytes=VMEM_LIMIT),
        cost_estimate=pl.CostEstimate(
            flops=2 * share * depth * width,
            bytes_accessed=2 * (share * (depth + width) + depth * width),
            transcendentals=0,
        ),
    )(rows_in, weight)


def local_states(half, near, far, near_rows, far_rows, head_count, head_size):
    share = near.shape[0]
    decay_block = near_rows.shape[1] // LANES - 1

    def kernel(half_ref, nk, nv, fk, fv, near_decay, far_decay, state_ref, running_ref):
        h = pl.program_id(0)
        mine = half_ref[0]

        @pl.when(h == 0)
        def _():
            source = lax.broadcasted_iota(jnp.int32, (share, share), 0)
            target = lax.broadcasted_iota(jnp.int32, (share, share), 1)
            upto = jnp.where(source <= target, 1.0, 0.0).astype(BF16)

            def sums(ref):
                logs = ref[...].astype(F32).T[:head_count, :].astype(BF16)
                return mm(logs, upto)

            running_ref[mine] = sums(near_decay)
            running_ref[1 - mine] = sums(far_decay)
            running_ref[1] = running_ref[1] + running_ref[0][:, share - 1 :]

        @pl.when(h < head_count)
        def _():
            last = running_ref[1, pl.ds(h, 1), :][:, share - 1 :]
            total = None
            for key_ref, value_ref, place in ((nk, nv, mine), (fk, fv, 1 - mine)):
                row = running_ref[place, pl.ds(h, 1), :]
                high, low = split(key_ref[...].T.astype(F32) * jnp.exp(last - row))
                values = value_ref[...]
                term = mm(high, values) + mm(low, values)
                total = term if total is None else total + term
            state_ref[0] = total

        @pl.when(h == head_count)
        def _():
            state_ref[...] = jnp.zeros_like(state_ref)
            state_ref[0, :head_count, :] = jnp.broadcast_to(
                running_ref[1][:, share - 1 :], (head_count, head_size)
            )

    last_head = head_count - 1

    def block(shift):
        return pl.BlockSpec(
            (share, head_size), lambda h: (0, shift + jnp.minimum(h, last_head))
        )

    decay_spec = pl.BlockSpec((share, LANES), lambda h: (0, decay_block))
    return pl.pallas_call(
        kernel,
        grid=(head_count + 1,),
        in_specs=[
            SMEM_SPEC,
            block(0),
            block(head_count),
            block(0),
            block(head_count),
            decay_spec,
            decay_spec,
        ],
        out_specs=[
            pl.BlockSpec((1, head_size, head_size), lambda h: (h, 0, 0)),
            pl.BlockSpec((2, head_count, share), lambda h: (0, 0, 0)),
        ],
        out_shape=[
            jax.ShapeDtypeStruct((head_count + 1, head_size, head_size), F32),
            jax.ShapeDtypeStruct((2, head_count, share), F32),
        ],
        compiler_params=pltpu.CompilerParams(vmem_limit_bytes=VMEM_LIMIT),
        cost_estimate=pl.CostEstimate(
            flops=8 * share * head_size * head_size * head_count,
            bytes_accessed=near.size * 4 + head_count * head_size * head_size * 4,
            transcendentals=2 * share * head_count,
        ),
    )(half, near, near, far, far, near_rows, far_rows)


def chain_outputs(half, near_q, far_q, near, far, running, incoming, first_head, here, head_count, head_size, capacity, rows):
    share = near.shape[0]
    group = share // capacity

    def kernel(half_ref, nq, fq, nk, fk, nv, fv, running_ref, incoming_ref, out_ref, q_s, k_s, v_s, o_s):
        h = pl.program_id(0) + first_head
        mine = half_ref[0]
        for scratch, near_ref, far_ref in ((q_s, nq, fq), (k_s, nk, fk), (v_s, nv, fv)):
            scratch[mine] = near_ref[...]
            scratch[1 - mine] = far_ref[...]
        state = incoming_ref[0]
        up = lax.broadcasted_iota(jnp.int32, (rows, rows), 0)
        across = lax.broadcasted_iota(jnp.int32, (rows, rows), 1)
        lower = up >= across
        previous = jnp.zeros((1, 1), F32)
        for side in range(2):
            running_row = running_ref[side, pl.ds(h, 1), :]
            for c in range(share // rows):
                span = slice(c * rows, (c + 1) * rows)
                query, key, value = q_s[side, span, :], k_s[side, span, :], v_s[side, span, :]
                row = running_row[:, span]
                wide = jnp.broadcast_to(row, (rows, rows))
                tall = wide.T
                weights = jnp.where(lower, jnp.exp(jnp.minimum(tall - wide, 0.0)), 0.0)
                scores, scores_low = split(mm_nt(query, key) * weights)
                state_high, state_low = split(state)
                grown = jnp.exp(tall[:, :head_size] - previous)
                earlier = (mm(query, state_high) + mm(query, state_low)) * grown
                outputs = mm(scores, value) + mm(scores_low, value) + earlier
                mean_square = jnp.mean(outputs * outputs, axis=-1, keepdims=True)
                o_s[side, span, :] = (outputs * lax.rsqrt(mean_square + 1e-06)).astype(BF16)
                ending = row[:, rows - 1 :]
                if side == 0 or (c + 1) * rows < share:
                    faded, faded_low = split(key.T.astype(F32) * jnp.exp(ending - row))
                    state = (
                        jnp.exp(ending - previous) * state
                        + mm(faded, value)
                        + mm(faded_low, value)
                    )
                previous = ending
        for b, place in enumerate((mine, 1 - mine)):
            for k in range(group):
                out_ref[k, b] = o_s[place, k * capacity : (k + 1) * capacity, :]

    def block(shift):
        return pl.BlockSpec((share, head_size), lambda h: (0, shift + first_head + h))

    return pl.pallas_call(
        kernel,
        grid=(here,),
        in_specs=[
            SMEM_SPEC,
            block(0),
            block(0),
            block(0),
            block(0),
            block(head_count),
            block(head_count),
            pl.BlockSpec(running.shape, lambda h: (0, 0, 0)),
            pl.BlockSpec((1, head_size, head_size), lambda h: (first_head + h, 0, 0)),
        ],
        out_specs=pl.BlockSpec((group, 2, capacity, head_size), lambda h: (0, 0, 0, h)),
        out_shape=jax.ShapeDtypeStruct((group, 2, capacity, here * head_size), BF16),
        scratch_shapes=[pltpu.VMEM((2, share, head_size), BF16) for _ in range(4)],
        compiler_params=pltpu.CompilerParams(vmem_limit_bytes=VMEM_LIMIT),
        cost_estimate=pl.CostEstimate(
            flops=2 * here * share * head_size * (6 * rows + 8 * head_size),
            bytes_accessed=16 * share * here * head_size,
            transcendentals=2 * here * share * rows,
        ),
    )(half, near_q, far_q, near, far, near, far, running, incoming)


def partner_sums(high, low, returned):
    group, _, capacity, width = returned.shape
    rows, share = high.shape[1:]
    tile = min(512, width)

    def kernel(high_ref, low_ref, returned_ref, out_ref):
        data = returned_ref[...].reshape(share, tile)
        out_ref[...] = (mm(high_ref[...], data) + mm(low_ref[...], data)).astype(BF16)

    gates = pl.BlockSpec((None, rows, share), lambda i: (1, 0, 0))
    return pl.pallas_call(
        kernel,
        grid=(width // tile,),
        in_specs=[
            gates,
            gates,
            pl.BlockSpec((group, None, capacity, tile), lambda i: (0, 1, 0, i)),
        ],
        out_specs=pl.BlockSpec((rows, tile), lambda i: (0, i)),
        out_shape=jax.ShapeDtypeStruct((rows, width), BF16),
        compiler_params=pltpu.CompilerParams(vmem_limit_bytes=VMEM_LIMIT),
        cost_estimate=pl.CostEstimate(
            flops=4 * rows * share * width,
            bytes_accessed=2 * width * (rows + share),
            transcendentals=0,
        ),
    )(high, low, returned)


def finish(high, low, returned, partner, mixed, first_column, full_width):
    group, _, capacity, width = returned.shape
    rows, share = high.shape[1:]
    tile = min(512, width)
    first = first_column // tile

    def kernel(*refs):
        high_ref, low_ref, returned_ref, partner_ref = refs[:4]
        data = returned_ref[...].reshape(share, tile)
        total = mm(high_ref[...], data) + mm(low_ref[...], data)
        refs[-1][...] = (total + partner_ref[...].astype(F32)).astype(BF16)

    gates = pl.BlockSpec((None, rows, share), lambda i: (0, 0, 0))
    in_specs = [
        gates,
        gates,
        pl.BlockSpec((group, None, capacity, tile), lambda i: (0, 0, 0, i)),
        pl.BlockSpec((rows, tile), lambda i: (0, i)),
    ]
    args = [high, low, returned, partner]
    aliases = {}
    if mixed is not None:
        in_specs.append(pl.BlockSpec(memory_space=pl.ANY))
        args.append(mixed)
        aliases = {4: 0}
    return pl.pallas_call(
        kernel,
        grid=(width // tile,),
        in_specs=in_specs,
        out_specs=pl.BlockSpec((rows, tile), lambda i: (0, first + i)),
        out_shape=jax.ShapeDtypeStruct((rows, full_width), BF16),
        input_output_aliases=aliases,
        compiler_params=pltpu.CompilerParams(vmem_limit_bytes=VMEM_LIMIT),
        cost_estimate=pl.CostEstimate(
            flops=4 * rows * share * width,
            bytes_accessed=2 * width * (2 * rows + share),
            transcendentals=0,
        ),
    )(*args)


def earlier_state(states, axis, head_count):
    size = lax.axis_size(axis)
    place = lax.axis_index(axis)
    total, total_log = states[:head_count], states[head_count, :head_count, 0]
    found = jnp.zeros_like(total)
    found_log = jnp.zeros_like(total_log)
    step = 1
    while step < size:
        last = step * 2 >= size
        if last:
            pairs = [(i, i + step) for i in range(size - step) if not i & step]
        else:
            pairs = [(i, i ^ step) for i in range(size)]
        planes = jnp.concatenate(
            [total, jnp.zeros((1,) + total.shape[1:], F32).at[0, :head_count, :].set(total_log[:, None])]
        ) if step > 1 else states
        other = lax.ppermute(planes, axis, pairs)
        other_total, other_log = other[:head_count], other[head_count, :head_count, 0]
        upper = (place & step) != 0
        found = found + jnp.where(upper, jnp.exp(found_log), 0.0)[:, None, None] * other_total
        found_log = found_log + jnp.where(upper, other_log, 0.0)
        if not last:
            mine = jnp.where(upper, 1.0, jnp.exp(other_log))[:, None, None]
            theirs = jnp.where(upper, jnp.exp(total_log), 1.0)[:, None, None]
            total = mine * total + theirs * other_total
            total_log = total_log + other_log
        step *= 2
    return found


def on_device(tokens, queries, log_decay, route_ids, gate_weights, kv_weight):
    tok_rows, model_width = tokens.shape
    head_count = log_decay.shape[1]
    head_size = model_width // head_count
    top = route_ids.shape[1]
    members = lax.axis_size("mem")
    capacity = 3 * tok_rows * top // (2 * members)
    group = members // 2
    share = group * capacity
    rows = math.gcd(share, 128)
    half = (lax.axis_index("mem") // group).astype(jnp.int32).reshape(1)
    across = [(i, (i + group) % members) for i in range(members)]
    sides = [list(range(group)), list(range(group, members))]

    def cross(array):
        return lax.ppermute(array, "mem", across)

    def swap(array):
        sent = array.reshape((group, -1) + array.shape[1:] if array.ndim == 2 else array.shape)
        return lax.all_to_all(
            sent, "mem", split_axis=0, concat_axis=0, axis_index_groups=sides, tiled=True
        ).reshape(array.shape)

    facts = jnp.concatenate(
        [
            route_ids.T.astype(F32),
            gate_weights.T,
            jnp.zeros((FACT_PAD, tok_rows), F32),
            log_decay.T.astype(F32),
        ],
        axis=0,
    )
    far_facts = cross(facts)
    far_tokens = cross(tokens)
    near_rows = swap(dispatch(half, facts, tokens, top, members, capacity, head_count))
    near = project(near_rows, kv_weight[0])
    far_rows = swap(dispatch(half, far_facts, far_tokens, top, members, capacity, head_count))
    later_queries, far_tokens = lax.optimization_barrier((queries, far_tokens))
    far_queries = cross(later_queries)
    near_q = dispatch(half, facts, queries, top, members, capacity, 0)
    near_q, far_rows = lax.optimization_barrier((near_q, far_rows))
    near_q = swap(near_q)
    far = project(far_rows, kv_weight[0])
    states, running = local_states(half, near, far, near_rows, far_rows, head_count, head_size)
    incoming = earlier_state(states, "tm", head_count)
    high, low = gate_matrices(half, facts, far_facts, top, members, capacity)
    far_q = swap(dispatch(half, far_facts, far_queries, top, members, capacity, 0))
    mixed = None
    first = 0
    for here in HEAD_PARTS:
        normed = chain_outputs(
            half, near_q, far_q, near, far, running, incoming,
            first, here, head_count, head_size, capacity, rows,
        )
        returned = swap(normed)
        partner = cross(partner_sums(high, low, returned))
        mixed = finish(high, low, returned, partner, mixed, first * head_size, model_width)
        first += here
    return mixed


def solution(mesh):
    placed = (
        P(("tm", "mem"), None),
        P(("tm", "mem"), None),
        P(("tm", "mem"), None),
        P(("tm", "mem"), None),
        P(("tm", "mem"), None),
        P("mem", None, None),
    )
    return jax.shard_map(
        on_device, mesh=mesh, in_specs=placed, out_specs=P(("tm", "mem"), None), check_vma=False
    )
```

time: 273 us -> 301 us (1.10)
  Pallas kernels: 46.9 us -> 73.6 us
  matrix products: 17.6 us -> 0 us
  waiting for transfers between devices: 150 us -> 164 us
  blocking collectives: 13.8 us -> 0 us
  starting transfers between devices: 26.4 us -> 37.9 us
    ppermute x0 -> x5, waiting for transfers between devices: none -> 112 us  [cross(): return lax.ppermute(array, 'mem', across)]
    all_to_all x5 -> x6, waiting for transfers between devices: 127 us -> 28.1 us  [swap(): lax.all_to_all(sent, 'mem', split_axis=0, concat_axis=0, axis_index_group...]
    pallas_call x7 -> x14, Pallas kernels: 46.9 us -> 73.6 us  [the longest x2 27 us: chain_outputs(): pl.pallas_call(kernel, grid=(here,), in_specs=[SMEM_SPEC, block(0), block...]
    dot_general x1 -> x0, matrix products: 17.6 us -> none  [on_device(): jnp.dot(chain_x, kv_weight[0], preferred_element_type=F32).astype(BF16)]
    all_to_all x1 -> x0, blocking collectives: 13.8 us -> none  [on_device(): lax.all_to_all(send_decay, 'mem', split_axis=0, concat_axis=0, tiled=True)]
    ppermute x0 -> x5, starting transfers between devices: none -> 7.85 us  [cross(): return lax.ppermute(array, 'mem', across)]
    all_to_all x5 -> x6, starting transfers between devices: 21.9 us -> 25.6 us  [swap(): lax.all_to_all(sent, 'mem', split_axis=0, concat_axis=0, axis_index_group...]
    unnamed x28 -> x32, local copies, waits for them, and re-layouts: 11.9 us -> 14.7 us
  transfers between devices with their start and end apart: 7 -> 13, of which waited for: 5 -> 6; matrix products, arithmetic and copies ran while one was open for 9% -> 2% of each run, Pallas kernels for 15% -> 19%
where the time goes in v2:
time: 301 us; the launch traced here: 299 us
  waiting for transfers between devices  164 us (54%)
  Pallas kernels  73.6 us (24%)
  starting transfers between devices  37.9 us (13%)
  local copies, waits for them, and re-layouts  14.8 us (5%)
  other arithmetic  8.53 us (3%)
    ppermute x5, waiting for transfers between devices, cross(): return lax.ppermute(array, 'mem', across)  112 us
    all_to_all x6, waiting for transfers between devices, swap(): lax.all_to_all(sent, 'mem', split_axis=0, concat_axis=0, axis_index_group...  28.1 us
    pallas_call x2, Pallas kernels, chain_outputs(): pl.pallas_call(kernel, grid=(here,), in_specs=[SMEM_SPEC, block(0), block...  27 us
    all_to_all x6, starting transfers between devices, swap(): lax.all_to_all(sent, 'mem', split_axis=0, concat_axis=0, axis_index_group...  25.6 us
    ppermute x2, waiting for transfers between devices, earlier_state(): other = lax.ppermute(planes, axis, pairs)  23.8 us
    pallas_call x2, Pallas kernels, project(): pl.pallas_call(kernel, grid=(width // tile,), in_specs=[pl.BlockSpec((sha...  23.6 us
    unnamed x32, local copies, waits for them, and re-layouts  14.7 us
    pallas_call x1, Pallas kernels, local_states(): pl.pallas_call(kernel, grid=(head_count + 1,), in_specs=[SMEM_SPEC, block...  9.86 us
  transfers between devices with their start and end apart: 13, of which 6 were waited for; matrix products, arithmetic and copies ran while one was open for 2% of the time, Pallas kernels for 19%

profile of v2, /device:TPU:0, one launch (start us, length us, event | category | flops | bytes accessed | tf_op | source)
XLA Modules:
  0.0 299.2 jit_solution(15815547198757262359)
XLA Ops:
  0.0 0.7 convert_bitcast_fusion
  0.7 0.7 convert_bitcast_fusion.1
  1.4 0.1 pad.9.clone
  1.5 0.8 pad_maximum_fusion.1.facts_ref
  2.2 1.2 copy-done.13
  3.4 2.0 shard_map.68
  5.5 5.4 %all-to-all-start.3 = ((bf16[4,96,2176]{2,1,0:T(8,128)(2,1)}), bf16[4,96,2176]{2,1,0:T(8,128)(2,1)S(1)}, u32[]{:S(2)}, u32[]{:S(2)}) async-start(bf16[4,96,2176]{2,1,0:T(8,128)(2,1)} %bitcast.10), calls=%async_computation.3 | async-start | bytes 3342336 | tf_op jit(solution)/shard_map/all_to_all | solution.py:418
  10.9 2.6 collective-permute-start.1
  13.5 0.3 collective-permute-start
  13.8 46.2 %collective-permute-done.partner_ref.facts_ref = f32[24,256]{1,0:T(8,128)S(1)} collective-permute-done((f32[24,256]{1,0:T(8,128)S(1)}, f32[24,256]{1,0:T(8,128)S(1)}, u32[]{:S(2)}, u32[]{:S(2)}) %collective-permute-start) | collective-permute-done | bytes 24608 | tf_op jit(solution)/shard_map/ppermute | solution.py:414
  60.1 0.0 collective-permute-done.1.data_ref
  60.1 0.8 shard_map.66
  60.9 1.2 copy-done.9
  62.1 0.0 all-to-all-done.3
  62.1 1.2 copy-done.5
  63.2 3.6 %all-to-all-start = ((bf16[4,96,2176]{2,1,0:T(8,128)(2,1)}), bf16[4,96,2176]{2,1,0:T(8,128)(2,1)S(1)}, u32[]{:S(2)}, u32[]{:S(2)}) async-start(bf16[4,96,2176]{2,1,0:T(8,128)(2,1)} %bitcast.19), calls=%async_computation | async-start | bytes 3342336 | tf_op jit(solution)/shard_map/all_to_all | solution.py:418
  66.8 2.9 collective-permute-start.2
  69.7 44.7 %collective-permute-done.2.data_ref = bf16[256,2048]{1,0:T(8,128)(2,1)S(1)} collective-permute-done((bf16[256,2048]{1,0:T(8,128)(2,1)}, bf16[256,2048]{1,0:T(8,128)(2,1)S(1)}, u32[]{:S(2)}, u32[]{:S(2)}) %collective-permute-start.2) | collective-permute-done | bytes 1048608 | tf_op jit(solution)/shard_map/ppermute | solution.py:414
  114.4 1.9 shard_map.67
  116.3 0.0 all-to-all-done
  116.3 1.3 copy-done.7
  117.6 4.3 %all-to-all-start.2 = ((bf16[4,96,2048]{2,1,0:T(8,128)(2,1)}), bf16[4,96,2048]{2,1,0:T(8,128)(2,1)}, u32[]{:S(2)}, u32[]{:S(2)}) async-start(bf16[4,96,2048]{2,1,0:T(8,128)(2,1)} %bitcast.8), calls=%async_computation.2 | async-start | bytes 3145728 | tf_op jit(solution)/shard_map/all_to_all | solution.py:418
  121.9 0.0 copy-done.15
  121.9 0.0 copy-start.6
  121.9 0.7 shard_map.65
  122.7 1.2 copy-done.10
  123.9 11.9 %shard_map.69.nk.nv = bf16[384,4096]{1,0:T(8,128)(2,1)S(1)} custom-call(bf16[384,2176]{1,0:T(8,128)(2,1)S(1)} %bitcast.15, bf16[2048,4096]{1,0:T(8,128)(2,1)} %bitcast.22), custom_call_target="tpu_custom_call" | custom-call | flops 6442450944 | bytes 21495808 | tf_op jit(solution)/shard_map/pallas_call | solution.py:130
  135.8 0.0 copy-done.8
  135.8 11.8 %shard_map.70.fk.fv = bf16[384,4096]{1,0:T(8,128)(2,1)S(1)} custom-call(bf16[384,2176]{1,0:T(8,128)(2,1)S(1)} %bitcast.17, bf16[2048,4096]{1,0:T(8,128)(2,1)} %bitcast.23), custom_call_target="tpu_custom_call" | custom-call | flops 6442450944 | bytes 21495808 | tf_op jit(solution)/shard_map/pallas_call | solution.py:130
  147.5 9.9 %shard_map.71 = (f32[17,128,128]{2,1,0:T(8,128)}, f32[2,16,384]{2,1,0:T(8,128)S(1)}) custom-call(s32[1]{0:T(128)} %bitcast.half_ref, bf16[384,4096]{1,0:T(8,128)(2,1)S(1)} %shard_map.69.nk.nv, bf16[384,4096]{1,0:T(8,128)(2,1)S(1)} %shard_map.69.nk.nv, bf16[384,4096]{1,0:T(8,128)(2,1)S(1)} %shard_map.70.fk.fv, bf16[384,4096]{1,0:T(8,128)(2,1)S(1)} %shard_map.70.fk.fv, ...), custom_call_target="tpu_custom_call" | custom-call | flops 805306368 | bytes 7340032 | tf_op jit(solution)/shard_map/pallas_call | solution.py:197
  157.4 0.0 collective-permute-start.3
  157.4 0.0 all-to-all-done.2
  157.4 4.4 %all-to-all-start.1 = ((bf16[4,96,2048]{2,1,0:T(8,128)(2,1)}), bf16[4,96,2048]{2,1,0:T(8,128)(2,1)}, u32[]{:S(2)}, u32[]{:S(2)}) async-start(bf16[4,96,2048]{2,1,0:T(8,128)(2,1)} %bitcast.20), calls=%async_computation.1 | async-start | bytes 3145728 | tf_op jit(solution)/shard_map/all_to_all | solution.py:418
  161.8 0.0 collective-permute-done.3
  161.8 0.9 select_reduce_fusion.2
  162.7 1.7 multiply_add_fusion
  164.4 0.1 scatter.8
  164.5 1.1 pad_maximum_fusion
  165.6 4.5 %collective-permute-start.4 = (f32[17,128,128]{2,1,0:T(8,128)}, f32[17,128,128]{2,1,0:T(8,128)}, u32[]{:S(2)}, u32[]{:S(2)}) collective-permute-start(f32[17,128,128]{2,1,0:T(8,128)} %pad_maximum_fusion), channel_id=1, source_target_pairs={{0,16},{8,24},{1,17},{9,25},{2,18},{10,26},{3,19},{11,27},{4,20},{... | collective-permute-start | bytes 3342344 | tf_op jit(solution)/shard_map/ppermute | solution.py:385
  170.1 23.8 %collective-permute-done.4 = f32[17,128,128]{2,1,0:T(8,128)} collective-permute-done((f32[17,128,128]{2,1,0:T(8,128)}, f32[17,128,128]{2,1,0:T(8,128)}, u32[]{:S(2)}, u32[]{:S(2)}) %collective-permute-start.4) | collective-permute-done | bytes 1114144 | tf_op jit(solution)/shard_map/ppermute | solution.py:385
  193.9 2.7 fusion.incoming_ref
  196.6 0.0 all-to-all-done.1
  196.6 1.9 copy-done.1
  198.5 1.2 copy-done.3
  199.7 13.5 %shard_map.74 = bf16[4,2,96,1024]{3,2,1,0:T(8,128)(2,1)S(1)} custom-call(s32[1]{0:T(128)} %bitcast.half_ref, bf16[384,2048]{1,0:T(8,128)(2,1)} %bitcast.7.nq, bf16[384,2048]{1,0:T(8,128)(2,1)} %bitcast.9.fq, bf16[384,4096]{1,0:T(8,128)(2,1)S(1)} %shard_map.69.nk.nv, bf16[384,4096]{1,0:T(8,128)(2,1)S(1)} %copy-done.1, bf16[384,4096]{1,0:T(8,128)(2,1)S(1)} %shard_map.69.nk.nv, ...), custom_call_target="tpu_custom_call" | custom-call | flops 1409286144 | bytes 6291456 | tf_op jit(solution)/shard_map/pallas_call | solution.py:273
  213.2 1.2 copy-done.12
  214.4 4.3 %all-to-all-start.5 = ((bf16[4,2,96,1024]{3,2,1,0:T(8,128)(2,1)}), bf16[4,2,96,1024]{3,2,1,0:T(8,128)(2,1)}, u32[]{:S(2)}, u32[]{:S(2)}) async-start(bf16[4,2,96,1024]{3,2,1,0:T(8,128)(2,1)} %copy-done.12), calls=%async_computation.5 | async-start | bytes 3145728 | tf_op jit(solution)/shard_map/all_to_all | solution.py:418
  218.8 1.9 copy-done.2
  220.7 1.2 copy-done.4
  221.9 13.5 %shard_map.72 = bf16[4,2,96,1024]{3,2,1,0:T(8,128)(2,1)S(1)} custom-call(s32[1]{0:T(128)} %bitcast.half_ref, bf16[384,2048]{1,0:T(8,128)(2,1)} %bitcast.7.nq, bf16[384,2048]{1,0:T(8,128)(2,1)} %bitcast.9.fq, bf16[384,4096]{1,0:T(8,128)(2,1)S(1)} %shard_map.69.nk.nv, bf16[384,4096]{1,0:T(8,128)(2,1)S(1)} %copy-done.2, bf16[384,4096]{1,0:T(8,128)(2,1)S(1)} %shard_map.69.nk.nv, ...), custom_call_target="tpu_custom_call" | custom-call | flops 1409286144 | bytes 6291456 | tf_op jit(solution)/shard_map/pallas_call | solution.py:273
  235.4 0.0 copy-start.11
  235.4 1.1 copy-done.11
  236.6 1.8 all-to-all-done.5.returned_ref.refs_2_
  238.4 3.6 %all-to-all-start.4 = ((bf16[4,2,96,1024]{3,2,1,0:T(8,128)(2,1)}), bf16[4,2,96,1024]{3,2,1,0:T(8,128)(2,1)S(1)}, u32[]{:S(2)}, u32[]{:S(2)}) async-start(bf16[4,2,96,1024]{3,2,1,0:T(8,128)(2,1)} %copy-done.11), calls=%async_computation.4 | async-start | bytes 3145728 | tf_op jit(solution)/shard_map/all_to_all | solution.py:418
  241.9 0.4 shard_map.64
  242.4 1.9 shard_map.75
  244.3 2.0 collective-permute-start.6
  246.3 26.3 %all-to-all-done.4.returned_ref.refs_2_ = bf16[4,2,96,1024]{3,2,1,0:T(8,128)(2,1)S(1)} async-done(((bf16[4,2,96,1024]{3,2,1,0:T(8,128)(2,1)}), bf16[4,2,96,1024]{3,2,1,0:T(8,128)(2,1)S(1)}, u32[]{:S(2)}, u32[]{:S(2)}) %all-to-all-start.4) | async-done | bytes 1572896 | tf_op jit(solution)/shard_map/all_to_all | solution.py:418
  272.5 1.0 shard_map.73
  273.5 0.1 collective-permute-start.5
  273.6 0.0 collective-permute-done.6.refs_3_
  273.6 2.6 shard_map.76.refs_4_
  276.2 21.3 %collective-permute-done.5.refs_3_ = bf16[256,1024]{1,0:T(8,128)(2,1)S(1)} collective-permute-done((bf16[256,1024]{1,0:T(8,128)(2,1)S(1)}, bf16[256,1024]{1,0:T(8,128)(2,1)S(1)}, u32[]{:S(2)}, u32[]{:S(2)}) %collective-permute-start.5) | collective-permute-done | bytes 524320 | tf_op jit(solution)/shard_map/ppermute | solution.py:414
  297.6 1.7 shard_map.77
  (19 shorter events, 0.0 us)
Async XLA Ops:
  2.2 1.2 copy-start.13
  5.5 5.4 %copy-start.14 = (bf16[256,2048]{1,0:T(8,128)(2,1)S(1)}, bf16[256,2048]{1,0:T(8,128)(2,1)}, u32[]{:S(2)}) copy-start(bf16[256,2048]{1,0:T(8,128)(2,1)} %data_ref.3) | copy-start | bytes 3145732
  5.5 56.6 %all-to-all-start.3 = ((bf16[4,96,2176]{2,1,0:T(8,128)(2,1)}), bf16[4,96,2176]{2,1,0:T(8,128)(2,1)S(1)}, u32[]{:S(2)}, u32[]{:S(2)}) async-start(bf16[4,96,2176]{2,1,0:T(8,128)(2,1)} %bitcast.10), calls=%async_computation.3 | async-start | bytes 3342336 | tf_op jit(solution)/shard_map/all_to_all | solution.py:418
  10.9 49.2 %collective-permute-start.1 = (bf16[256,2048]{1,0:T(8,128)(2,1)S(1)}, bf16[256,2048]{1,0:T(8,128)(2,1)S(1)}, u32[]{:S(2)}, u32[]{:S(2)}) collective-permute-start(bf16[256,2048]{1,0:T(8,128)(2,1)S(1)} %copy-done.14), channel_id=1, source_target_pairs={{0,4},{1,5},{2,6},{3,7},{4,0},{5,1},{6,2},{7,3},{8,12},{9,13},{10,... | collective-permute-start | bytes 3145736 | tf_op jit(solution)/shard_map/ppermute | solution.py:414
  13.5 46.6 %collective-permute-start = (f32[24,256]{1,0:T(8,128)S(1)}, f32[24,256]{1,0:T(8,128)S(1)}, u32[]{:S(2)}, u32[]{:S(2)}) collective-permute-start(f32[24,256]{1,0:T(8,128)S(1)} %pad_maximum_fusion.1.facts_ref), channel_id=1, source_target_pairs={{0,4},{1,5},{2,6},{3,7},{4,0},{5,1},{6,2},{7,3},{8,12},{9,13},{10,... | collective-permute-start | bytes 73736 | tf_op jit(solution)/shard_map/ppermute | solution.py:414
  60.9 1.2 copy-start.9
  62.1 1.2 copy-start.5
  63.2 53.0 %all-to-all-start = ((bf16[4,96,2176]{2,1,0:T(8,128)(2,1)}), bf16[4,96,2176]{2,1,0:T(8,128)(2,1)S(1)}, u32[]{:S(2)}, u32[]{:S(2)}) async-start(bf16[4,96,2176]{2,1,0:T(8,128)(2,1)} %bitcast.19), calls=%async_computation | async-start | bytes 3342336 | tf_op jit(solution)/shard_map/all_to_all | solution.py:418
  66.8 47.6 %collective-permute-start.2 = (bf16[256,2048]{1,0:T(8,128)(2,1)}, bf16[256,2048]{1,0:T(8,128)(2,1)S(1)}, u32[]{:S(2)}, u32[]{:S(2)}) collective-permute-start(bf16[256,2048]{1,0:T(8,128)(2,1)} %data_ref.2), channel_id=1, source_target_pairs={{0,4},{1,5},{2,6},{3,7},{4,0},{5,1},{6,2},{7,3},{8,12},{9,13},{10,... | collective-permute-start | bytes 3145736 | tf_op jit(solution)/shard_map/ppermute | solution.py:414
  116.3 1.3 copy-start.7
  116.3 5.6 %copy-start.15 = (bf16[256,2048]{1,0:T(8,128)(2,1)S(1)}, bf16[256,2048]{1,0:T(8,128)(2,1)}, u32[]{:S(2)}) copy-start(bf16[256,2048]{1,0:T(8,128)(2,1)} %data_ref.2) | copy-start | bytes 3145732
  117.6 39.9 %all-to-all-start.2 = ((bf16[4,96,2048]{2,1,0:T(8,128)(2,1)}), bf16[4,96,2048]{2,1,0:T(8,128)(2,1)}, u32[]{:S(2)}, u32[]{:S(2)}) async-start(bf16[4,96,2048]{2,1,0:T(8,128)(2,1)} %bitcast.8), calls=%async_computation.2 | async-start | bytes 3145728 | tf_op jit(solution)/shard_map/all_to_all | solution.py:418
  121.9 2.0 copy-start.6
  122.7 1.2 copy-start.10
  123.9 11.9 %copy-start.8 = (bf16[4,96,2176]{2,1,0:T(8,128)(2,1)S(1)}, bf16[4,96,2176]{2,1,0:T(8,128)(2,1)}, u32[]{:S(2)}) copy-start(bf16[4,96,2176]{2,1,0:T(8,128)(2,1)} %copy-done.7) | copy-start | bytes 5013508
  147.5 9.9 %copy-start = (bf16[384,4096]{1,0:T(8,128)(2,1)}, bf16[384,4096]{1,0:T(8,128)(2,1)S(1)}, u32[]{:S(2)}) copy-start(bf16[384,4096]{1,0:T(8,128)(2,1)S(1)} %shard_map.70.fk.fv) | copy-start | bytes 9437188
  157.4 4.4 %collective-permute-start.3 = (f32[17,128,128]{2,1,0:T(8,128)}, f32[17,128,128]{2,1,0:T(8,128)}, u32[]{:S(2)}, u32[]{:S(2)}) collective-permute-start(f32[17,128,128]{2,1,0:T(8,128)} %get-tuple-element.30), channel_id=1, source_target_pairs={{0,8},{8,0},{16,24},{24,16},{1,9},{9,1},{17,25},{25,17},{2,10},{10... | collective-permute-start | bytes 3342344 | tf_op jit(solution)/shard_map/ppermute | solution.py:385
  157.4 39.2 %all-to-all-start.1 = ((bf16[4,96,2048]{2,1,0:T(8,128)(2,1)}), bf16[4,96,2048]{2,1,0:T(8,128)(2,1)}, u32[]{:S(2)}, u32[]{:S(2)}) async-start(bf16[4,96,2048]{2,1,0:T(8,128)(2,1)} %bitcast.20), calls=%async_computation.1 | async-start | bytes 3145728 | tf_op jit(solution)/shard_map/all_to_all | solution.py:418
  165.6 28.3 %collective-permute-start.4 = (f32[17,128,128]{2,1,0:T(8,128)}, f32[17,128,128]{2,1,0:T(8,128)}, u32[]{:S(2)}, u32[]{:S(2)}) collective-permute-start(f32[17,128,128]{2,1,0:T(8,128)} %pad_maximum_fusion), channel_id=1, source_target_pairs={{0,16},{8,24},{1,17},{9,25},{2,18},{10,26},{3,19},{11,27},{4,20},{... | collective-permute-start | bytes 3342344 | tf_op jit(solution)/shard_map/ppermute | solution.py:385
  196.6 1.9 copy-start.1
  198.5 1.2 copy-start.3
  213.2 1.3 copy-start.12
  214.4 23.9 %all-to-all-start.5 = ((bf16[4,2,96,1024]{3,2,1,0:T(8,128)(2,1)}), bf16[4,2,96,1024]{3,2,1,0:T(8,128)(2,1)}, u32[]{:S(2)}, u32[]{:S(2)}) async-start(bf16[4,2,96,1024]{3,2,1,0:T(8,128)(2,1)} %copy-done.12), calls=%async_computation.5 | async-start | bytes 3145728 | tf_op jit(solution)/shard_map/all_to_all | solution.py:418
  218.8 1.9 copy-start.2
  220.7 1.2 copy-start.4
  235.4 1.1 copy-start.11
  238.4 34.2 %all-to-all-start.4 = ((bf16[4,2,96,1024]{3,2,1,0:T(8,128)(2,1)}), bf16[4,2,96,1024]{3,2,1,0:T(8,128)(2,1)S(1)}, u32[]{:S(2)}, u32[]{:S(2)}) async-start(bf16[4,2,96,1024]{3,2,1,0:T(8,128)(2,1)} %copy-done.11), calls=%async_computation.4 | async-start | bytes 3145728 | tf_op jit(solution)/shard_map/all_to_all | solution.py:418
  244.3 29.3 %collective-permute-start.6 = (bf16[256,1024]{1,0:T(8,128)(2,1)S(1)}, bf16[256,1024]{1,0:T(8,128)(2,1)S(1)}, u32[]{:S(2)}, u32[]{:S(2)}) collective-permute-start(bf16[256,1024]{1,0:T(8,128)(2,1)S(1)} %shard_map.75), channel_id=1, source_target_pairs={{0,4},{1,5},{2,6},{3,7},{4,0},{5,1},{6,2},{7,3},{8,12},{9,13},{10,... | collective-permute-start | bytes 1572872 | tf_op jit(solution)/shard_map/ppermute | solution.py:414
  273.5 24.0 %collective-permute-start.5 = (bf16[256,1024]{1,0:T(8,128)(2,1)S(1)}, bf16[256,1024]{1,0:T(8,128)(2,1)S(1)}, u32[]{:S(2)}, u32[]{:S(2)}) collective-permute-start(bf16[256,1024]{1,0:T(8,128)(2,1)S(1)} %shard_map.73), channel_id=1, source_target_pairs={{0,4},{1,5},{2,6},{3,7},{4,0},{5,1},{6,2},{7,3},{8,12},{9,13},{10,... | collective-permute-start | bytes 1572872 | tf_op jit(solution)/shard_map/ppermute | solution.py:414

commit v3 on v2

--- a/solution.py
+++ b/solution.py
@@ -7,9 +7,9 @@
 from jax.experimental.pallas import tpu as pltpu
 from jax.sharding import PartitionSpec as P
 
+
 F32 = jnp.float32
 BF16 = jnp.bfloat16
-VMEM_LIMIT = 40 << 20
 LANES = 128
 FACT_PAD = 4
 HEAD_PARTS = (8, 8)
@@ -82,7 +82,6 @@
         in_specs=[SMEM_SPEC, VMEM_SPEC, VMEM_SPEC],
         out_specs=VMEM_SPEC,
         out_shape=jax.ShapeDtypeStruct((share, full), BF16),
-        compiler_params=pltpu.CompilerParams(vmem_limit_bytes=VMEM_LIMIT),
         cost_estimate=pl.CostEstimate(
             flops=2 * share * rows * width,
             bytes_accessed=2 * width * (rows + share),
@@ -110,7 +109,6 @@
         in_specs=[SMEM_SPEC, VMEM_SPEC, VMEM_SPEC],
         out_specs=[VMEM_SPEC, VMEM_SPEC],
         out_shape=[shape, shape],
-        compiler_params=pltpu.CompilerParams(vmem_limit_bytes=VMEM_LIMIT),
         cost_estimate=pl.CostEstimate(
             flops=4 * rows * rows * members,
             bytes_accessed=8 * rows * share,
@@ -136,7 +134,6 @@
         ],
         out_specs=pl.BlockSpec((share, tile), lambda i: (0, i)),
         out_shape=jax.ShapeDtypeStruct((share, width), BF16),
-        compiler_params=pltpu.CompilerParams(vmem_limit_bytes=VMEM_LIMIT),
         cost_estimate=pl.CostEstimate(
             flops=2 * share * depth * width,
             bytes_accessed=2 * (share * (depth + width) + depth * width),
@@ -214,7 +211,6 @@
             jax.ShapeDtypeStruct((head_count + 1, head_size, head_size), F32),
             jax.ShapeDtypeStruct((2, head_count, share), F32),
         ],
-        compiler_params=pltpu.CompilerParams(vmem_limit_bytes=VMEM_LIMIT),
         cost_estimate=pl.CostEstimate(
             flops=8 * share * head_size * head_size * head_count,
             bytes_accessed=near.size * 4 + head_count * head_size * head_size * 4,
@@ -287,7 +283,6 @@
         out_specs=pl.BlockSpec((group, 2, capacity, head_size), lambda h: (0, 0, 0, h)),
         out_shape=jax.ShapeDtypeStruct((group, 2, capacity, here * head_size), BF16),
         scratch_shapes=[pltpu.VMEM((2, share, head_size), BF16) for _ in range(4)],
-        compiler_params=pltpu.CompilerParams(vmem_limit_bytes=VMEM_LIMIT),
         cost_estimate=pl.CostEstimate(
             flops=2 * here * share * head_size * (6 * rows + 8 * head_size),
             bytes_accessed=16 * share * here * head_size,
@@ -316,7 +311,6 @@
         ],
         out_specs=pl.BlockSpec((rows, tile), lambda i: (0, i)),
         out_shape=jax.ShapeDtypeStruct((rows, width), BF16),
-        compiler_params=pltpu.CompilerParams(vmem_limit_bytes=VMEM_LIMIT),
         cost_estimate=pl.CostEstimate(
             flops=4 * rows * share * width,
             bytes_accessed=2 * width * (rows + share),
@@ -357,7 +351,6 @@
         out_specs=pl.BlockSpec((rows, tile), lambda i: (0, first + i)),
         out_shape=jax.ShapeDtypeStruct((rows, full_width), BF16),
         input_output_aliases=aliases,
-        compiler_params=pltpu.CompilerParams(vmem_limit_bytes=VMEM_LIMIT),
         cost_estimate=pl.CostEstimate(
             flops=4 * rows * share * width,
             bytes_accessed=2 * width * (2 * rows + share),
@@ -428,21 +421,19 @@
         ],
         axis=0,
     )
+    sizes = (top, members, capacity)
     far_facts = cross(facts)
     far_tokens = cross(tokens)
-    near_rows = swap(dispatch(half, facts, tokens, top, members, capacity, head_count))
+    near_rows = swap(dispatch(half, facts, tokens, *sizes, head_count))
     near = project(near_rows, kv_weight[0])
-    far_rows = swap(dispatch(half, far_facts, far_tokens, top, members, capacity, head_count))
-    later_queries, far_tokens = lax.optimization_barrier((queries, far_tokens))
-    far_queries = cross(later_queries)
-    near_q = dispatch(half, facts, queries, top, members, capacity, 0)
-    near_q, far_rows = lax.optimization_barrier((near_q, far_rows))
-    near_q = swap(near_q)
+    far_rows = swap(dispatch(half, far_facts, far_tokens, *sizes, head_count))
+    far_queries = cross(queries)
+    near_q = swap(dispatch(half, facts, queries, *sizes, 0))
     far = project(far_rows, kv_weight[0])
     states, running = local_states(half, near, far, near_rows, far_rows, head_count, head_size)
     incoming = earlier_state(states, "tm", head_count)
-    high, low = gate_matrices(half, facts, far_facts, top, members, capacity)
-    far_q = swap(dispatch(half, far_facts, far_queries, top, members, capacity, 0))
+    high, low = gate_matrices(half, facts, far_facts, *sizes)
+    far_q = swap(dispatch(half, far_facts, far_queries, *sizes, 0))
     mixed = None
     first = 0
     for here in HEAD_PARTS:
@@ -466,6 +457,7 @@
         P(("tm", "mem"), None),
         P("mem", None, None),
     )
+
     return jax.shard_map(
         on_device, mesh=mesh, in_specs=placed, out_specs=P(("tm", "mem"), None), check_vma=False
     )

time: 301 us -> 285 us (0.947)
  waiting for transfers between devices: 164 us -> 137 us
  Pallas kernels: 73.6 us -> 93.6 us
  local copies, waits for them, and re-layouts: 14.8 us -> 8.33 us
    ppermute x5, waiting for transfers between devices: 112 us -> 72 us  [cross(): return lax.ppermute(array, 'mem', across)]
    all_to_all x6, waiting for transfers between devices: 28.1 us -> 43.9 us  [swap(): lax.all_to_all(sent, 'mem', split_axis=0, concat_axis=0, axis_index_group...]
    pallas_call x4, Pallas kernels: 5.49 us -> 12.8 us  [dispatch(): pl.pallas_call(kernel, in_specs=[SMEM_SPEC, VMEM_SPEC, VMEM_SPEC], out_sp...]
    unnamed x32 -> x22, local copies, waits for them, and re-layouts: 14.7 us -> 8.17 us
    pallas_call x1, Pallas kernels: 9.86 us -> 13.3 us  [local_states(): pl.pallas_call(kernel, grid=(head_count + 1,), in_specs=[SMEM_SPEC, block...]
    pallas_call x2, Pallas kernels: 23.6 us -> 26.9 us  [project(): pl.pallas_call(kernel, grid=(width // tile,), in_specs=[pl.BlockSpec((sha...]
  transfers between devices with their start and end apart: 13 -> 13, of which waited for: 6 -> 7; matrix products, arithmetic and copies ran while one was open for 2% -> 2% of each run, Pallas kernels for 19% -> 26%
where the time goes in v3:
time: 285 us; the launch traced here: 283 us
  waiting for transfers between devices  137 us (48%)
  Pallas kernels  93.6 us (33%)
  starting transfers between devices  35.6 us (12%)
  local copies, waits for them, and re-layouts  8.33 us (3%)
  other arithmetic  8.1 us (3%)
    ppermute x5, waiting for transfers between devices, cross(): return lax.ppermute(array, 'mem', across)  72 us
    all_to_all x6, waiting for transfers between devices, swap(): lax.all_to_all(sent, 'mem', split_axis=0, concat_axis=0, axis_index_group...  43.9 us
    pallas_call x2, Pallas kernels, chain_outputs(): pl.pallas_call(kernel, grid=(here,), in_specs=[SMEM_SPEC, block(0), block...  27.4 us
    pallas_call x2, Pallas kernels, project(): pl.pallas_call(kernel, grid=(width // tile,), in_specs=[pl.BlockSpec((sha...  26.9 us
    all_to_all x6, starting transfers between devices, swap(): lax.all_to_all(sent, 'mem', split_axis=0, concat_axis=0, axis_index_group...  24.5 us
    ppermute x2, waiting for transfers between devices, earlier_state(): other = lax.ppermute(planes, axis, pairs)  21.2 us
    pallas_call x1, Pallas kernels, local_states(): pl.pallas_call(kernel, grid=(head_count + 1,), in_specs=[SMEM_SPEC, block...  13.3 us
    pallas_call x4, Pallas kernels, dispatch(): pl.pallas_call(kernel, in_specs=[SMEM_SPEC, VMEM_SPEC, VMEM_SPEC], out_sp...  12.8 us
  transfers between devices with their start and end apart: 13, of which 7 were waited for; matrix products, arithmetic and copies ran while one was open for 2% of the time, Pallas kernels for 26%

profile of v3, /device:TPU:0, one launch (start us, length us, event | category | flops | bytes accessed | tf_op | source)
XLA Modules:
  0.0 282.9 jit_solution(16073978954212899177)
XLA Ops:
  0.0 0.7 convert_bitcast_fusion
  0.7 0.7 convert_bitcast_fusion.1
  1.4 0.1 pad.9.clone
  1.5 1.4 pad_maximum_fusion.1.facts_ref
  2.8 3.2 %shard_map.67 = bf16[384,2176]{1,0:T(8,128)(2,1)} custom-call(s32[1]{0:T(128)} %bitcast.half_ref, f32[24,256]{1,0:T(8,128)} %pad_maximum_fusion.1.facts_ref, bf16[256,2048]{1,0:T(8,128)(2,1)} %data_ref.3), custom_call_target="tpu_custom_call" | custom-call | flops 402653184 | bytes 2621440 | tf_op jit(solution)/shard_map/pallas_call | solution.py:80
  6.0 0.0 copy-start.5
  6.0 0.0 copy-start.9
  6.1 5.4 %all-to-all-start.2 = ((bf16[4,96,2176]{2,1,0:T(8,128)(2,1)}), bf16[4,96,2176]{2,1,0:T(8,128)(2,1)S(1)}, u32[]{:S(2)}, u32[]{:S(2)}) async-start(bf16[4,96,2176]{2,1,0:T(8,128)(2,1)} %bitcast.21), calls=%async_computation.2 | async-start | bytes 3342336 | tf_op jit(solution)/shard_map/all_to_all | solution.py:411
  11.5 0.0 copy-done.5
  11.5 2.6 collective-permute-start.2
  14.1 0.0 copy-done.9
  14.1 0.3 collective-permute-start
  14.4 46.2 %collective-permute-done.partner_ref.facts_ref = f32[24,256]{1,0:T(8,128)S(1)} collective-permute-done((f32[24,256]{1,0:T(8,128)S(1)}, f32[24,256]{1,0:T(8,128)S(1)}, u32[]{:S(2)}, u32[]{:S(2)}) %collective-permute-start) | collective-permute-done | bytes 24608 | tf_op jit(solution)/shard_map/ppermute | solution.py:407
  60.6 0.0 copy-start.10
  60.6 0.0 collective-permute-done.2.data_ref
  60.6 0.6 copy-done.10
  61.2 3.3 %shard_map.69 = bf16[384,2176]{1,0:T(8,128)(2,1)} custom-call(s32[1]{0:T(128)} %bitcast.half_ref, f32[24,256]{1,0:T(8,128)} %copy-done.10, bf16[256,2048]{1,0:T(8,128)(2,1)} %collective-permute-done.2.data_ref), custom_call_target="tpu_custom_call" | custom-call | flops 402653184 | bytes 2621440 | tf_op jit(solution)/shard_map/pallas_call | solution.py:80
  64.5 0.0 all-to-all-done.2
  64.5 1.3 copy-done.4
  65.8 4.4 %all-to-all-start.3 = ((bf16[4,96,2176]{2,1,0:T(8,128)(2,1)}), bf16[4,96,2176]{2,1,0:T(8,128)(2,1)}, u32[]{:S(2)}, u32[]{:S(2)}) async-start(bf16[4,96,2176]{2,1,0:T(8,128)(2,1)} %bitcast.22), calls=%async_computation.3 | async-start | bytes 3342336 | tf_op jit(solution)/shard_map/all_to_all | solution.py:411
  70.2 3.1 %shard_map.65 = bf16[384,2048]{1,0:T(8,128)(2,1)} custom-call(s32[1]{0:T(128)} %bitcast.half_ref, f32[24,256]{1,0:T(8,128)} %pad_maximum_fusion.1.facts_ref, bf16[256,2048]{1,0:T(8,128)(2,1)} %data_ref.2), custom_call_target="tpu_custom_call" | custom-call | flops 402653184 | bytes 2621440 | tf_op jit(solution)/shard_map/pallas_call | solution.py:80
  73.3 16.6 %all-to-all-done.3 = bf16[4,96,2176]{2,1,0:T(8,128)(2,1)} async-done(((bf16[4,96,2176]{2,1,0:T(8,128)(2,1)}), bf16[4,96,2176]{2,1,0:T(8,128)(2,1)}, u32[]{:S(2)}, u32[]{:S(2)}) %all-to-all-start.3) | async-done | bytes 1671200 | tf_op jit(solution)/shard_map/all_to_all | solution.py:411
  89.9 3.7 %all-to-all-start = ((bf16[4,96,2048]{2,1,0:T(8,128)(2,1)}), bf16[4,96,2048]{2,1,0:T(8,128)(2,1)S(1)}, u32[]{:S(2)}, u32[]{:S(2)}) async-start(bf16[4,96,2048]{2,1,0:T(8,128)(2,1)} %bitcast.24), calls=%async_computation | async-start | bytes 3145728 | tf_op jit(solution)/shard_map/all_to_all | solution.py:411
  93.6 0.0 copy-done.6
  93.6 2.3 collective-permute-start.1
  95.9 13.5 %shard_map.68.nk.nv = bf16[384,4096]{1,0:T(8,128)(2,1)} custom-call(bf16[384,2176]{1,0:T(8,128)(2,1)} %bitcast.19, bf16[2048,4096]{1,0:T(8,128)(2,1)} %bitcast.26), custom_call_target="tpu_custom_call" | custom-call | flops 6442450944 | bytes 21495808 | tf_op jit(solution)/shard_map/pallas_call | solution.py:128
  109.4 13.4 %shard_map.70.fk.fv = bf16[384,4096]{1,0:T(8,128)(2,1)} custom-call(bf16[384,2176]{1,0:T(8,128)(2,1)} %bitcast.12.rows_ref.far_decay, bf16[2048,4096]{1,0:T(8,128)(2,1)} %bitcast.27), custom_call_target="tpu_custom_call" | custom-call | flops 6442450944 | bytes 21495808 | tf_op jit(solution)/shard_map/pallas_call | solution.py:128
  122.8 13.3 %shard_map.71 = (f32[17,128,128]{2,1,0:T(8,128)}, f32[2,16,384]{2,1,0:T(8,128)}) custom-call(s32[1]{0:T(128)} %bitcast.half_ref, bf16[384,4096]{1,0:T(8,128)(2,1)} %shard_map.68.nk.nv, bf16[384,4096]{1,0:T(8,128)(2,1)} %shard_map.68.nk.nv, bf16[384,4096]{1,0:T(8,128)(2,1)} %shard_map.70.fk.fv, bf16[384,4096]{1,0:T(8,128)(2,1)} %shard_map.70.fk.fv, ...), custom_call_target="tpu_custom_call" | custom-call | flops 805306368 | bytes 7340032 | tf_op jit(solution)/shard_map/pallas_call | solution.py:194
  136.1 0.0 collective-permute-start.3
  136.1 5.2 %collective-permute-done.1.data_ref = bf16[256,2048]{1,0:T(8,128)(2,1)} collective-permute-done((bf16[256,2048]{1,0:T(8,128)(2,1)S(1)}, bf16[256,2048]{1,0:T(8,128)(2,1)}, u32[]{:S(2)}, u32[]{:S(2)}) %collective-permute-start.1) | collective-permute-done | bytes 1048608 | tf_op jit(solution)/shard_map/ppermute | solution.py:407
  141.3 3.1 %shard_map.66 = bf16[384,2048]{1,0:T(8,128)(2,1)} custom-call(s32[1]{0:T(128)} %bitcast.half_ref, f32[24,256]{1,0:T(8,128)} %copy-done.10, bf16[256,2048]{1,0:T(8,128)(2,1)} %collective-permute-done.1.data_ref), custom_call_target="tpu_custom_call" | custom-call | flops 402653184 | bytes 2621440 | tf_op jit(solution)/shard_map/pallas_call | solution.py:80
  144.5 0.0 all-to-all-done
  144.5 1.2 copy-done
  145.7 3.6 %all-to-all-start.1 = ((bf16[4,96,2048]{2,1,0:T(8,128)(2,1)}), bf16[4,96,2048]{2,1,0:T(8,128)(2,1)S(1)}, u32[]{:S(2)}, u32[]{:S(2)}) async-start(bf16[4,96,2048]{2,1,0:T(8,128)(2,1)} %bitcast.23), calls=%async_computation.1 | async-start | bytes 3145728 | tf_op jit(solution)/shard_map/all_to_all | solution.py:411
  149.3 0.0 collective-permute-done.3
  149.3 0.9 select_reduce_fusion.2
  150.2 1.7 multiply_add_fusion
  151.9 0.1 scatter.8
  152.0 0.1 pad_maximum_fusion
  152.1 4.5 %collective-permute-start.4 = (f32[17,128,128]{2,1,0:T(8,128)S(1)}, f32[17,128,128]{2,1,0:T(8,128)}, u32[]{:S(2)}, u32[]{:S(2)}) collective-permute-start(f32[17,128,128]{2,1,0:T(8,128)S(1)} %pad_maximum_fusion), channel_id=1, source_target_pairs={{0,16},{8,24},{1,17},{9,25},{2,18},{10,26},{3,19},{11,27},{4,20},{... | collective-permute-start | bytes 3342344 | tf_op jit(solution)/shard_map/ppermute | solution.py:378
  156.6 21.2 %collective-permute-done.4 = f32[17,128,128]{2,1,0:T(8,128)} collective-permute-done((f32[17,128,128]{2,1,0:T(8,128)S(1)}, f32[17,128,128]{2,1,0:T(8,128)}, u32[]{:S(2)}, u32[]{:S(2)}) %collective-permute-start.4) | collective-permute-done | bytes 1114144 | tf_op jit(solution)/shard_map/ppermute | solution.py:378
  177.8 2.7 fusion.incoming_ref
  180.5 0.0 all-to-all-done.1
  180.5 1.1 copy-done.1
  181.7 13.6 %shard_map.74 = bf16[4,2,96,1024]{3,2,1,0:T(8,128)(2,1)} custom-call(s32[1]{0:T(128)} %bitcast.half_ref, bf16[384,2048]{1,0:T(8,128)(2,1)} %bitcast.15, bf16[384,2048]{1,0:T(8,128)(2,1)} %bitcast.17, bf16[384,4096]{1,0:T(8,128)(2,1)} %shard_map.68.nk.nv, bf16[384,4096]{1,0:T(8,128)(2,1)} %shard_map.70.fk.fv, bf16[384,4096]{1,0:T(8,128)(2,1)} %shard_map.68.nk.nv, ...), custom_call_target="tpu_custom_call" | custom-call | flops 1409286144 | bytes 6291456 | tf_op jit(solution)/shard_map/pallas_call | solution.py:269
  195.3 3.9 %all-to-all-start.5 = ((bf16[4,2,96,1024]{3,2,1,0:T(8,128)(2,1)}), bf16[4,2,96,1024]{3,2,1,0:T(8,128)(2,1)S(1)}, u32[]{:S(2)}, u32[]{:S(2)}) async-start(bf16[4,2,96,1024]{3,2,1,0:T(8,128)(2,1)} %shard_map.74), calls=%async_computation.5 | async-start | bytes 3145728 | tf_op jit(solution)/shard_map/all_to_all | solution.py:411
  199.2 13.8 %shard_map.72 = bf16[4,2,96,1024]{3,2,1,0:T(8,128)(2,1)} custom-call(s32[1]{0:T(128)} %bitcast.half_ref, bf16[384,2048]{1,0:T(8,128)(2,1)} %bitcast.16, bf16[384,2048]{1,0:T(8,128)(2,1)} %bitcast.18, bf16[384,4096]{1,0:T(8,128)(2,1)} %shard_map.68.nk.nv, bf16[384,4096]{1,0:T(8,128)(2,1)} %shard_map.70.fk.fv, bf16[384,4096]{1,0:T(8,128)(2,1)} %shard_map.68.nk.nv, ...), custom_call_target="tpu_custom_call" | custom-call | flops 1409286144 | bytes 6291456 | tf_op jit(solution)/shard_map/pallas_call | solution.py:269
  212.9 3.0 %all-to-all-done.5.returned_ref.refs_2_ = bf16[4,2,96,1024]{3,2,1,0:T(8,128)(2,1)S(1)} async-done(((bf16[4,2,96,1024]{3,2,1,0:T(8,128)(2,1)}), bf16[4,2,96,1024]{3,2,1,0:T(8,128)(2,1)S(1)}, u32[]{:S(2)}, u32[]{:S(2)}) %all-to-all-start.5) | async-done | bytes 1572896 | tf_op jit(solution)/shard_map/all_to_all | solution.py:411
  215.9 1.2 copy-done.3
  217.1 3.6 %all-to-all-start.4 = ((bf16[4,2,96,1024]{3,2,1,0:T(8,128)(2,1)}), bf16[4,2,96,1024]{3,2,1,0:T(8,128)(2,1)S(1)}, u32[]{:S(2)}, u32[]{:S(2)}) async-start(bf16[4,2,96,1024]{3,2,1,0:T(8,128)(2,1)} %shard_map.72), calls=%async_computation.4 | async-start | bytes 3145728 | tf_op jit(solution)/shard_map/all_to_all | solution.py:411
  220.7 2.1 shard_map.64
  222.8 2.7 shard_map.75
  225.5 1.4 collective-permute-start.6
  226.9 24.3 %all-to-all-done.4.returned_ref.refs_2_ = bf16[4,2,96,1024]{3,2,1,0:T(8,128)(2,1)S(1)} async-done(((bf16[4,2,96,1024]{3,2,1,0:T(8,128)(2,1)}), bf16[4,2,96,1024]{3,2,1,0:T(8,128)(2,1)S(1)}, u32[]{:S(2)}, u32[]{:S(2)}) %all-to-all-start.4) | async-done | bytes 1572896 | tf_op jit(solution)/shard_map/all_to_all | solution.py:411
  251.3 1.1 copy-done.2
  252.4 2.8 shard_map.73
  255.2 0.0 collective-permute-start.5
  255.2 0.0 collective-permute-done.6.refs_3_
  255.2 0.0 copy-start.7
  255.2 0.8 copy-done.7
  256.0 2.8 shard_map.76.refs_4_
  258.7 20.6 %collective-permute-done.5.refs_3_ = bf16[256,1024]{1,0:T(8,128)(2,1)S(1)} collective-permute-done((bf16[256,1024]{1,0:T(8,128)(2,1)}, bf16[256,1024]{1,0:T(8,128)(2,1)S(1)}, u32[]{:S(2)}, u32[]{:S(2)}) %collective-permute-start.5) | collective-permute-done | bytes 524320 | tf_op jit(solution)/shard_map/ppermute | solution.py:407
  279.3 0.8 copy-done.8
  280.1 2.8 shard_map.77
  (9 shorter events, 0.0 us)
Async XLA Ops:
  6.0 5.4 %copy-start.5 = (bf16[256,2048]{1,0:T(8,128)(2,1)S(1)}, bf16[256,2048]{1,0:T(8,128)(2,1)}, u32[]{:S(2)}) copy-start(bf16[256,2048]{1,0:T(8,128)(2,1)} %data_ref.3) | copy-start | bytes 3145732
  6.0 8.0 %copy-start.9 = (f32[24,256]{1,0:T(8,128)S(1)}, f32[24,256]{1,0:T(8,128)}, u32[]{:S(2)}) copy-start(f32[24,256]{1,0:T(8,128)} %pad_maximum_fusion.1.facts_ref) | copy-start | bytes 73732
  6.1 58.5 %all-to-all-start.2 = ((bf16[4,96,2176]{2,1,0:T(8,128)(2,1)}), bf16[4,96,2176]{2,1,0:T(8,128)(2,1)S(1)}, u32[]{:S(2)}, u32[]{:S(2)}) async-start(bf16[4,96,2176]{2,1,0:T(8,128)(2,1)} %bitcast.21), calls=%async_computation.2 | async-start | bytes 3342336 | tf_op jit(solution)/shard_map/all_to_all | solution.py:411
  11.5 49.2 %collective-permute-start.2 = (bf16[256,2048]{1,0:T(8,128)(2,1)S(1)}, bf16[256,2048]{1,0:T(8,128)(2,1)}, u32[]{:S(2)}, u32[]{:S(2)}) collective-permute-start(bf16[256,2048]{1,0:T(8,128)(2,1)S(1)} %copy-done.5), channel_id=1, source_target_pairs={{0,4},{1,5},{2,6},{3,7},{4,0},{5,1},{6,2},{7,3},{8,12},{9,13},{10,... | collective-permute-start | bytes 3145736 | tf_op jit(solution)/shard_map/ppermute | solution.py:407
  14.1 46.6 %collective-permute-start = (f32[24,256]{1,0:T(8,128)S(1)}, f32[24,256]{1,0:T(8,128)S(1)}, u32[]{:S(2)}, u32[]{:S(2)}) collective-permute-start(f32[24,256]{1,0:T(8,128)S(1)} %copy-done.9), channel_id=1, source_target_pairs={{0,4},{1,5},{2,6},{3,7},{4,0},{5,1},{6,2},{7,3},{8,12},{9,13},{10,... | collective-permute-start | bytes 73736 | tf_op jit(solution)/shard_map/ppermute | solution.py:407
  60.6 0.6 copy-start.10
  64.5 1.3 copy-start.4
  65.8 24.1 %all-to-all-start.3 = ((bf16[4,96,2176]{2,1,0:T(8,128)(2,1)}), bf16[4,96,2176]{2,1,0:T(8,128)(2,1)}, u32[]{:S(2)}, u32[]{:S(2)}) async-start(bf16[4,96,2176]{2,1,0:T(8,128)(2,1)} %bitcast.22), calls=%async_computation.3 | async-start | bytes 3342336 | tf_op jit(solution)/shard_map/all_to_all | solution.py:411
  89.9 3.7 %copy-start.6 = (bf16[256,2048]{1,0:T(8,128)(2,1)S(1)}, bf16[256,2048]{1,0:T(8,128)(2,1)}, u32[]{:S(2)}) copy-start(bf16[256,2048]{1,0:T(8,128)(2,1)} %data_ref.2) | copy-start | bytes 3145732
  89.9 54.6 %all-to-all-start = ((bf16[4,96,2048]{2,1,0:T(8,128)(2,1)}), bf16[4,96,2048]{2,1,0:T(8,128)(2,1)S(1)}, u32[]{:S(2)}, u32[]{:S(2)}) async-start(bf16[4,96,2048]{2,1,0:T(8,128)(2,1)} %bitcast.24), calls=%async_computation | async-start | bytes 3145728 | tf_op jit(solution)/shard_map/all_to_all | solution.py:411
  93.6 47.7 %collective-permute-start.1 = (bf16[256,2048]{1,0:T(8,128)(2,1)S(1)}, bf16[256,2048]{1,0:T(8,128)(2,1)}, u32[]{:S(2)}, u32[]{:S(2)}) collective-permute-start(bf16[256,2048]{1,0:T(8,128)(2,1)S(1)} %copy-done.6), channel_id=1, source_target_pairs={{0,4},{1,5},{2,6},{3,7},{4,0},{5,1},{6,2},{7,3},{8,12},{9,13},{10,... | collective-permute-start | bytes 3145736 | tf_op jit(solution)/shard_map/ppermute | solution.py:407
  136.1 13.2 %collective-permute-start.3 = (f32[17,128,128]{2,1,0:T(8,128)}, f32[17,128,128]{2,1,0:T(8,128)}, u32[]{:S(2)}, u32[]{:S(2)}) collective-permute-start(f32[17,128,128]{2,1,0:T(8,128)} %get-tuple-element.24), channel_id=1, source_target_pairs={{0,8},{8,0},{16,24},{24,16},{1,9},{9,1},{17,25},{25,17},{2,10},{10... | collective-permute-start | bytes 3342344 | tf_op jit(solution)/shard_map/ppermute | solution.py:378
  144.5 1.2 copy-start
  145.7 34.8 %all-to-all-start.1 = ((bf16[4,96,2048]{2,1,0:T(8,128)(2,1)}), bf16[4,96,2048]{2,1,0:T(8,128)(2,1)S(1)}, u32[]{:S(2)}, u32[]{:S(2)}) async-start(bf16[4,96,2048]{2,1,0:T(8,128)(2,1)} %bitcast.23), calls=%async_computation.1 | async-start | bytes 3145728 | tf_op jit(solution)/shard_map/all_to_all | solution.py:411
  152.1 25.7 %collective-permute-start.4 = (f32[17,128,128]{2,1,0:T(8,128)S(1)}, f32[17,128,128]{2,1,0:T(8,128)}, u32[]{:S(2)}, u32[]{:S(2)}) collective-permute-start(f32[17,128,128]{2,1,0:T(8,128)S(1)} %pad_maximum_fusion), channel_id=1, source_target_pairs={{0,16},{8,24},{1,17},{9,25},{2,18},{10,26},{3,19},{11,27},{4,20},{... | collective-permute-start | bytes 3342344 | tf_op jit(solution)/shard_map/ppermute | solution.py:378
  180.5 1.1 copy-start.1
  195.3 20.6 %all-to-all-start.5 = ((bf16[4,2,96,1024]{3,2,1,0:T(8,128)(2,1)}), bf16[4,2,96,1024]{3,2,1,0:T(8,128)(2,1)S(1)}, u32[]{:S(2)}, u32[]{:S(2)}) async-start(bf16[4,2,96,1024]{3,2,1,0:T(8,128)(2,1)} %shard_map.74), calls=%async_computation.5 | async-start | bytes 3145728 | tf_op jit(solution)/shard_map/all_to_all | solution.py:411
  215.9 1.2 copy-start.3
  217.1 34.2 %all-to-all-start.4 = ((bf16[4,2,96,1024]{3,2,1,0:T(8,128)(2,1)}), bf16[4,2,96,1024]{3,2,1,0:T(8,128)(2,1)S(1)}, u32[]{:S(2)}, u32[]{:S(2)}) async-start(bf16[4,2,96,1024]{3,2,1,0:T(8,128)(2,1)} %shard_map.72), calls=%async_computation.4 | async-start | bytes 3145728 | tf_op jit(solution)/shard_map/all_to_all | solution.py:411
  225.5 29.7 %collective-permute-start.6 = (bf16[256,1024]{1,0:T(8,128)(2,1)}, bf16[256,1024]{1,0:T(8,128)(2,1)S(1)}, u32[]{:S(2)}, u32[]{:S(2)}) collective-permute-start(bf16[256,1024]{1,0:T(8,128)(2,1)} %shard_map.75), channel_id=1, source_target_pairs={{0,4},{1,5},{2,6},{3,7},{4,0},{5,1},{6,2},{7,3},{8,12},{9,13},{10,... | collective-permute-start | bytes 1572872 | tf_op jit(solution)/shard_map/ppermute | solution.py:407
  251.3 1.1 copy-start.2
  255.2 24.1 %collective-permute-start.5 = (bf16[256,1024]{1,0:T(8,128)(2,1)}, bf16[256,1024]{1,0:T(8,128)(2,1)S(1)}, u32[]{:S(2)}, u32[]{:S(2)}) collective-permute-start(bf16[256,1024]{1,0:T(8,128)(2,1)} %shard_map.73), channel_id=1, source_target_pairs={{0,4},{1,5},{2,6},{3,7},{4,0},{5,1},{6,2},{7,3},{8,12},{9,13},{10,... | collective-permute-start | bytes 1572872 | tf_op jit(solution)/shard_map/ppermute | solution.py:407
  255.2 0.8 copy-start.7
  279.3 0.8 copy-start.8
